TPU v7x, 32 devices: a whole 2x2x4 slice. The times are simulated.
32 devices in a mesh: row: 8 (over z, core), col: 4 (over y, x).
Axes of the slice: x: 2, y: 2, z: 4, core: 2. Of those that a mesh axis runs over, the one named last changes fastest.
Arguments:
- amplitudes: float32 [16, 16, 160, 160], P('row', 'col'), may hold values from -8 to 8, as said below
- vvvv: float32 [160, 160, 160, 160], P('row', None, 'col'), may hold values from -0.0390625 to 0.0390625
- hole_ints: float32 [16, 16, 16, 16], replicated, may hold values from -0.375 to 0.375
- exchange_ints: float32 [16, 16, 160, 160], P('row', None, 'col'), may hold values from -0.0024414062 to 0.0024414062
- fock_occ: float32 [16, 16], replicated, may hold values from -1.5 to 1.5
- fock_vir: float32 [160, 160], replicated, may hold values from -0.5 to 0.5
- eps_occ: float32 [16], replicated, may hold values from -2 to -0.5
- eps_vir: float32 [160], replicated, may hold values from 0.3 to 3
Outputs:
- update: float32 [16, 16, 160, 160], P('row', 'col')
Inputs may be any that keep to these rules, and one draw needn't show every extreme that they name: amplitudes[i, j, a, b] equals amplitudes[j, i, b, a].
All inputs are finite; a program needn't handle non-finite values.
Results may differ from a plain program's by a relative error of at most 0.000064.
Values sent between devices are 32-bit elements; how exact they have to be, the bound alone decides.
A program may use at most 256 MiB of HBM per device.

v0:
```python
import jax
import jax.numpy as jnp
from jax import lax
from jax.sharding import PartitionSpec as P

def on_device(amplitudes, vvvv, hole_ints, exchange_ints, fock_occ, fock_vir, eps_occ, eps_vir):
    high = lax.Precision.HIGH
    rows_n = lax.axis_size("row")
    cols_n = lax.axis_size("col")
    row = lax.axis_index("row")
    col = lax.axis_index("col")
    first_count, second_count, virtual = amplitudes.shape[:3]
    occupied = fock_occ.shape[0]
    pairs_n = occupied * occupied
    a_count = vvvv.shape[0]
    c_count = vvvv.shape[2]
    k_count = exchange_ints.shape[0]

    split = lax.all_to_all(amplitudes, "col", split_axis=2, concat_axis=1, tiled=True)
    split = split.reshape(first_count * occupied, c_count * virtual)
    gathered = lax.all_gather(split, "row", axis=0, tiled=True)
    gathered = gathered.reshape(occupied, occupied, c_count, virtual)

    chi_part = lax.dot_general(
        gathered, exchange_ints, (((2, 3), (2, 3)), ((), ())), precision=high
    )
    chi_part = chi_part.reshape(pairs_n, k_count * occupied).T
    chi_all = lax.all_gather(chi_part, ("row", "col"), axis=0)
    chi = chi_all.reshape(rows_n, cols_n, k_count * occupied, pairs_n).sum(axis=1)
    delta = jnp.eye(occupied, dtype=fock_occ.dtype)
    known = hole_ints - delta[:, None, :, None] * fock_occ[None, :, None, :]
    mixing = chi.reshape(pairs_n, pairs_n) + known.reshape(pairs_n, pairs_n)

    mine = lax.dynamic_slice_in_dim(gathered, row * a_count, a_count, axis=3)
    mine = mine.transpose(1, 0, 3, 2).reshape(pairs_n, a_count * c_count)
    placed = lax.all_gather(mine, "col", axis=0)
    placed = placed.reshape(cols_n, pairs_n, a_count, c_count).transpose(1, 2, 0, 3)
    placed = placed.reshape(pairs_n, a_count * virtual)

    part = lax.dot_general(gathered, vvvv, (((2, 3), (2, 3)), ((), ())), precision=high)
    part = part.transpose(1, 0, 2, 3).reshape(occupied, occupied, a_count * virtual)
    raw = lax.psum_scatter(part, "col", scatter_dimension=0, tiled=True)
    chosen = lax.dynamic_slice_in_dim(
        mixing.reshape(pairs_n, occupied, occupied), col * second_count, second_count, axis=2
    )
    chosen = chosen.transpose(0, 2, 1).reshape(pairs_n, second_count * occupied)
    hole = lax.dot_general(chosen, placed, (((0,), (0,)), ((), ())), precision=high)
    raw = raw + hole.reshape(raw.shape)
    raw = raw.reshape(second_count, rows_n, first_count, a_count * virtual)
    raw = raw.transpose(1, 2, 0, 3)
    raw = lax.all_to_all(raw, "row", split_axis=0, concat_axis=0, tiled=True)
    raw = raw.transpose(1, 2, 0, 3).reshape(first_count, second_count, virtual * virtual)

    ratio = second_count // first_count
    others = []
    for turn in range(ratio):
        route = []
        for r in range(rows_n):
            for q in range(cols_n):
                m = (r + turn) % ratio
                route.append((r * cols_n + q, (q * ratio + m) * cols_n + r // ratio))
        m = lax.rem(row + turn, ratio)
        block = lax.dynamic_slice_in_dim(raw, m * first_count, first_count, axis=1)
        others.append(lax.ppermute(block, ("row", "col"), route))
    stacked = jnp.stack(others)
    order = jnp.stack([lax.rem(row - m + ratio, ratio) for m in range(ratio)])
    other = stacked[order].reshape(ratio, first_count, first_count, virtual, virtual)
    other = other.transpose(2, 0, 1, 4, 3)
    other = other.reshape(first_count, second_count, virtual, virtual)
    total = raw.reshape(first_count, second_count, virtual, virtual) + other
    total = total + jnp.einsum("ijac,cb->ijab", amplitudes, fock_vir, precision=high)
    total = total + jnp.einsum("ac,ijcb->ijab", fock_vir, amplitudes, precision=high)
    energy_rows = lax.dynamic_slice_in_dim(eps_occ, row * first_count, first_count)
    energy_cols = lax.dynamic_slice_in_dim(eps_occ, col * second_count, second_count)
    denominator = (
        energy_rows[:, None, None, None]
        + energy_cols[None, :, None, None]
        - eps_vir[None, None, :, None]
        - eps_vir[None, None, None, :]
    )
    return total / denominator


def solution(mesh):
    in_specs = (
        P("row", "col", None, None),
        P("row", None, "col", None),
        P(),
        P("row", None, "col", None),
        P(),
        P(),
        P(),
        P(),
    )
    out_specs = P("row", "col", None, None)
    return jax.shard_map(
        on_device, mesh=mesh, in_specs=in_specs, out_specs=out_specs, check_vma=False
    )
```

profile of v0, /device:TPU:3, one launch (start us, length us, event | category | flops | bytes accessed | tf_op | source)
XLA Modules:
  0.0 432.6 jit_solution(12215672303684575956)
XLA Ops:
  6.5 2.2 copy.47
  8.7 18.8 %all_to_all.20 = f32[2,4,160,160]{3,1,0,2:T(4,128)S(1)} all-to-all(f32[2,4,160,160]{3,1,0,2:T(4,128)S(1)} %copy.47), channel_id=1, replica_groups=mesh['row'=8,'col'=4] {'col'}, dimensions={2} | all-to-all | bytes 1638400 | tf_op jit(solution)/shard_map/all_to_all | solution.py:19
  29.5 68.8 %all-gather.5.cloned.1.call-done = f32[256,6400]{1,0:T(8,128)} async-done(((f32[32,6400]{1,0:T(8,128)}), f32[256,6400]{1,0:T(8,128)}) %all-gather.5.cloned.1.call-update) | async-done | bytes 6553616 | tf_op jit(solution)/shard_map/all_gather | solution.py:21
  98.2 8.2 %copy.52 = f32[256,6400]{0,1:T(8,128)} copy(f32[256,6400]{1,0:T(8,128)} %all-gather.5.cloned.1.call-done) | data formatting | bytes 13107200 | tf_op jit(solution)/shard_map/all_gather | solution.py:21
  106.4 5.6 %fusion.13 = f32[32,256]{1,0:T(8,128)} fusion(f32[256,40,160]{0,2,1:T(8,128)} %bitcast.75, f32[32,40,160]{2,1,0:T(8,128)S(1)} %bitcast.87), kind=kOutput, calls=%fused_computation.16 | convolution fusion | flops 314572800 | bytes 7405568 | tf_op jit(solution)/shard_map/dot_general | solution.py:24
  112.1 11.0 %reshape.184 = f32[16,16,40,160]{3,2,1,0:T(8,128)} reshape(f32[256,6400]{1,0:T(8,128)} %all-gather.5.cloned.1.call-done) | data formatting | bytes 13107200 | tf_op jit(solution)/shard_map/reshape | solution.py:22
  123.1 7.8 %dynamic-slice_bitcast_fusion = f32[16,16,20,40]{2,3,0,1:T(8,128)} fusion(f32[16,16,40,160]{3,2,1,0:T(8,128)} %reshape.184, s32[]{:T(128)S(6)} %select_n.27), kind=kLoop, calls=%fused_computation.5 | loop fusion | bytes 1638404 | tf_op jit(solution)/shard_map/transpose | solution.py:35
  130.8 4.7 %copy.57 = f32[16,16,20,40]{3,2,1,0:T(8,128)S(1)} copy(f32[16,16,20,40]{2,3,0,1:T(8,128)} %dynamic-slice_bitcast_fusion) | data formatting | bytes 1638400 | tf_op jit(solution)/shard_map/transpose | solution.py:35
  137.2 2.4 copy.58
  139.8 129.2 %fusion.4 = f32[16,16,20,160]{3,0,2,1:T(8,128)} fusion(f32[20,160,40,160]{3,2,1,0:T(8,128)} %param.9, f32[16,16,40,160,1]{3,2,1,0,4:T(8,128)} %bitcast.76), kind=kOutput, calls=%fused_computation.7 | convolution fusion | flops 31457280000 | bytes 91750400 | tf_op jit(solution)/shard_map/dot_general | solution.py:40
  269.0 8.2 %copy.51 = f32[16,16,20,160]{3,2,1,0:T(8,128)} copy(f32[16,16,20,160]{3,0,2,1:T(8,128)} %fusion.4) | data formatting | bytes 6553600 | tf_op jit(solution)/shard_map/transpose | solution.py:41
  277.3 6.2 %reshape.185 = f32[16,16,3200]{2,1,0:T(8,128)} reshape(f32[16,16,20,160]{3,2,1,0:T(8,128)} %copy.51) | data formatting | bytes 6553600 | tf_op jit(solution)/shard_map/reshape | solution.py:41
  289.1 2.4 copy.59
  291.5 35.2 %reduce-scatter.2.cloned.1.call-done = f32[4,16,3200]{2,1,0:T(8,128)} async-done(((f32[16,16,3200]{2,1,0:T(8,128)}), f32[4,16,3200]{2,1,0:T(8,128)}) %reduce-scatter.2.cloned.1.call-update) | async-done | bytes 819216 | tf_op jit(solution)/shard_map/reduce_scatter | solution.py:42
  326.7 2.7 convolution_add_fusion
  330.7 5.6 %all-to-all-start.1 = ((f32[8,2,4,3200]{3,2,1,0:T(4,128)}), f32[8,2,4,3200]{3,2,1,0:T(4,128)S(1)}, u32[]{:S(2)}, u32[]{:S(2)}) async-start(f32[8,2,4,3200]{3,2,1,0:T(4,128)} %bitcast.22), calls=%async_computation.2 | async-start | bytes 1638400 | tf_op jit(solution)/shard_map/all_to_all | solution.py:51
  336.5 20.4 %all-to-all-done.1 = f32[8,2,4,3200]{3,2,1,0:T(4,128)S(1)} async-done(((f32[8,2,4,3200]{3,2,1,0:T(4,128)}), f32[8,2,4,3200]{3,2,1,0:T(4,128)S(1)}, u32[]{:S(2)}, u32[]{:S(2)}) %all-to-all-start.1) | async-done | bytes 819232 | tf_op jit(solution)/shard_map/all_to_all | solution.py:51
  357.4 2.2 collective-permute-start
  359.6 3.6 collective-permute-start.1
  365.1 40.7 %collective-permute-done = f32[2,2,25600]{2,1,0:T(2,128)S(1)} collective-permute-done((f32[2,2,25600]{2,1,0:T(2,128)S(1)}, f32[2,2,25600]{2,1,0:T(2,128)S(1)}, u32[]{:S(2)}, u32[]{:S(2)}) %collective-permute-start) | collective-permute-done | bytes 409632 | tf_op jit(solution)/shard_map/ppermute | solution.py:64
  405.8 9.5 %collective-permute-done.1 = f32[2,2,25600]{2,1,0:T(2,128)S(1)} collective-permute-done((f32[2,2,25600]{2,1,0:T(2,128)S(1)}, f32[2,2,25600]{2,1,0:T(2,128)S(1)}, u32[]{:S(2)}, u32[]{:S(2)}) %collective-permute-start.1) | collective-permute-done | bytes 409632 | tf_op jit(solution)/shard_map/ppermute | solution.py:64
  415.6 2.3 gather_fusion
  417.9 2.2 reshape.194
  421.8 2.4 convolution_add_fusion.1
  (49 shorter events, 17.3 us)
Async XLA Ops:
  6.5 415.2 %copy-start = (f32[160,160]{1,0:T(8,128)S(1)}, f32[160,160]{1,0:T(8,128)}, u32[]{:S(2)}) copy-start(f32[160,160]{1,0:T(8,128)} %param.13) | copy-start | bytes 307204
  6.5 91.7 %all-gather.5.cloned.1.call-start = ((), (), s32[]{:S(2)}) async-start(), calls=%async_computation.3 | async-start | bytes 7372800 | tf_op jit(solution)/shard_map/all_gather | solution.py:21
  29.4 77.0 %copy-start.3 = (f32[2,16,40,160]{3,2,1,0:T(8,128)S(1)}, f32[2,16,40,160]{3,2,1,0:T(8,128)}, u32[]{:S(2)}) copy-start(f32[2,16,40,160]{3,2,1,0:T(8,128)} %param.11) | copy-start | bytes 2457604
  29.4 257.5 %all-gather.9.cloned.1.call-start = ((), (), s32[]{:S(2)}) async-start(), calls=%async_computation.6 | async-start | bytes 1081344 | tf_op jit(solution)/shard_map/all_gather | solution.py:28
  112.0 177.0 %all-gather.7.cloned.1.call-start = ((), (), s32[]{:S(2)}) async-start(), calls=%async_computation.5 | async-start | bytes 4096000 | tf_op jit(solution)/shard_map/all_gather | solution.py:36
  139.6 187.1 %reduce-scatter.2.cloned.1.call-start = ((), (), s32[]{:S(2)}) async-start(), calls=%async_computation.4 | async-start | bytes 4096000 | tf_op jit(solution)/shard_map/reduce_scatter | solution.py:42
  283.5 1.6 copy-start.2
  283.5 1.6 copy-start.4
  329.4 6.8 %copy-start.6 = (f32[16]{0:T(128)S(1)}, f32[16]{0:T(128)}, u32[]{:S(2)}) copy-start(f32[16]{0:T(128)} %param.14) | copy-start | bytes 196
  330.7 32.5 %copy-start.5 = (f32[160]{0:T(256)S(1)}, f32[160]{0:T(256)}, u32[]{:S(2)}) copy-start(f32[160]{0:T(256)} %param.15) | copy-start | bytes 1924
  330.7 26.3 %all-to-all-start.1 = ((f32[8,2,4,3200]{3,2,1,0:T(4,128)}), f32[8,2,4,3200]{3,2,1,0:T(4,128)S(1)}, u32[]{:S(2)}, u32[]{:S(2)}) async-start(f32[8,2,4,3200]{3,2,1,0:T(4,128)} %bitcast.22), calls=%async_computation.2 | async-start | bytes 1638400 | tf_op jit(solution)/shard_map/all_to_all | solution.py:51
  357.4 48.4 %collective-permute-start = (f32[2,2,25600]{2,1,0:T(2,128)S(1)}, f32[2,2,25600]{2,1,0:T(2,128)S(1)}, u32[]{:S(2)}, u32[]{:S(2)}) collective-permute-start(f32[2,2,25600]{2,1,0:T(2,128)S(1)} %get-tuple-element.5), channel_id=1, source_target_pairs={{0,0},{1,8},{2,16},{3,24},{4,4},{5,12},{6,20},{7,28},{8,1},{9,9},{... | collective-permute-start | bytes 1228808 | tf_op jit(solution)/shard_map/ppermute | solution.py:64
  359.6 55.7 %collective-permute-start.1 = (f32[2,2,25600]{2,1,0:T(2,128)S(1)}, f32[2,2,25600]{2,1,0:T(2,128)S(1)}, u32[]{:S(2)}, u32[]{:S(2)}) collective-permute-start(f32[2,2,25600]{2,1,0:T(2,128)S(1)} %get-tuple-element.6), channel_id=1, source_target_pairs={{0,4},{1,12},{2,20},{3,28},{4,0},{5,8},{6,16},{7,24},{8,5},{9,13},... | collective-permute-start | bytes 1228808 | tf_op jit(solution)/shard_map/ppermute | solution.py:64
  417.9 3.9 copy-start.1
Sparse Core Ops, SparseCore 0:
  29.5 68.6 all-gather.4
  112.2 52.1 all-gather.8
  166.2 43.4 all-gather.6
  283.6 43.0 reduce-scatter.1
where the time goes:
time: 434 us; the launch traced here: 433 us
  waiting for transfers between devices  175 us (40%)
  matrix products  142 us (33%)
  local copies, waits for them, and re-layouts  70.2 us (16%)
  blocking collectives  18.8 us (4%)
  between operations  13.3 us (3%)
  starting transfers between devices  11.6 us (3%)
    dot_general x1, matrix products, on_device(): lax.dot_general(gathered, vvvv, (((2, 3), (2, 3)), ((), ())), precision=h...  129 us
    all_gather x1, waiting for transfers between devices, on_device(): gathered = lax.all_gather(split, 'row', axis=0, tiled=True)  68.8 us
    ppermute x2, waiting for transfers between devices, on_device(): others.append(lax.ppermute(block, ('row', 'col'), route))  50.2 us
    reduce_scatter x1, waiting for transfers between devices, on_device(): raw = lax.psum_scatter(part, 'col', scatter_dimension=0, tiled=True)  35.2 us
    all_to_all x1, waiting for transfers between devices, on_device(): raw = lax.all_to_all(raw, 'row', split_axis=0, concat_axis=0, tiled=True)  20.4 us
    all_to_all x1, blocking collectives, on_device(): lax.all_to_all(amplitudes, 'col', split_axis=2, concat_axis=1, tiled=True)  18.8 us
    transpose x2, local copies, waits for them, and re-layouts, on_device(): mine = mine.transpose(1, 0, 3, 2).reshape(pairs_n, a_count * c_count)  12.4 us
    reshape x1, local copies, waits for them, and re-layouts, on_device(): gathered = gathered.reshape(occupied, occupied, c_count, virtual)  11 us
  transfers between devices with their start and end apart: 7, of which 5 were waited for; matrix products, arithmetic and copies ran while one was open for 42% of the time, Pallas kernels for 0%

commit v1 on v0

v1 whole, which is shorter than its diff:
```python
import functools

import jax
import jax.numpy as jnp
from jax import lax
from jax.experimental import pallas as pl
from jax.experimental.pallas import tpu as pltpu
from jax.sharding import PartitionSpec as P

def finish(raw, amplitudes, fock_vir, eps_occ, eps_vir):
    high = lax.Precision.HIGH
    rows_n = lax.axis_size("row")
    cols_n = lax.axis_size("col")
    row = lax.axis_index("row")
    col = lax.axis_index("col")
    first_count, second_count, virtual = amplitudes.shape[:3]
    ratio = second_count // first_count
    others = []
    for turn in range(ratio):
        route = []
        for r in range(rows_n):
            for q in range(cols_n):
                m = (r + turn) % ratio
                route.append((r * cols_n + q, (q * ratio + m) * cols_n + r // ratio))
        m = lax.rem(row + turn, ratio)
        block = lax.dynamic_slice_in_dim(raw, m * first_count, first_count, axis=1)
        others.append(lax.ppermute(block, ("row", "col"), route))
    stacked = jnp.stack(others)
    order = jnp.stack([lax.rem(row - m + ratio, ratio) for m in range(ratio)])
    other = stacked[order].reshape(ratio, first_count, first_count, virtual, virtual)
    other = other.transpose(2, 0, 1, 4, 3)
    other = other.reshape(first_count, second_count, virtual, virtual)
    total = raw.reshape(first_count, second_count, virtual, virtual) + other
    total = total + jnp.einsum("ijac,cb->ijab", amplitudes, fock_vir, precision=high)
    total = total + jnp.einsum("ac,ijcb->ijab", fock_vir, amplitudes, precision=high)
    energy_rows = lax.dynamic_slice_in_dim(eps_occ, row * first_count, first_count)
    energy_cols = lax.dynamic_slice_in_dim(eps_occ, col * second_count, second_count)
    denominator = (
        energy_rows[:, None, None, None]
        + energy_cols[None, :, None, None]
        - eps_vir[None, None, :, None]
        - eps_vir[None, None, None, :]
    )
    return total / denominator


def plain(amplitudes, vvvv, hole_ints, exchange_ints, fock_occ, fock_vir, eps_occ, eps_vir):
    high = lax.Precision.HIGH
    rows_n = lax.axis_size("row")
    cols_n = lax.axis_size("col")
    row = lax.axis_index("row")
    col = lax.axis_index("col")
    first_count, second_count, virtual = amplitudes.shape[:3]
    occupied = fock_occ.shape[0]
    pairs_n = occupied * occupied
    a_count = vvvv.shape[0]
    c_count = vvvv.shape[2]
    k_count = exchange_ints.shape[0]

    split = lax.all_to_all(amplitudes, "col", split_axis=2, concat_axis=1, tiled=True)
    split = split.reshape(first_count * occupied, c_count * virtual)
    gathered = lax.all_gather(split, "row", axis=0, tiled=True)
    gathered = gathered.reshape(occupied, occupied, c_count, virtual)

    chi_part = lax.dot_general(
        gathered, exchange_ints, (((2, 3), (2, 3)), ((), ())), precision=high
    )
    chi_part = chi_part.reshape(pairs_n, k_count * occupied).T
    chi_all = lax.all_gather(chi_part, ("row", "col"), axis=0)
    chi = chi_all.reshape(rows_n, cols_n, k_count * occupied, pairs_n).sum(axis=1)
    delta = jnp.eye(occupied, dtype=fock_occ.dtype)
    known = hole_ints - delta[:, None, :, None] * fock_occ[None, :, None, :]
    mixing = chi.reshape(pairs_n, pairs_n) + known.reshape(pairs_n, pairs_n)

    mine = lax.dynamic_slice_in_dim(gathered, row * a_count, a_count, axis=3)
    mine = mine.transpose(1, 0, 3, 2).reshape(pairs_n, a_count * c_count)
    placed = lax.all_gather(mine, "col", axis=0)
    placed = placed.reshape(cols_n, pairs_n, a_count, c_count).transpose(1, 2, 0, 3)
    placed = placed.reshape(pairs_n, a_count * virtual)

    part = lax.dot_general(gathered, vvvv, (((2, 3), (2, 3)), ((), ())), precision=high)
    part = part.transpose(1, 0, 2, 3).reshape(occupied, occupied, a_count * virtual)
    raw = lax.psum_scatter(part, "col", scatter_dimension=0, tiled=True)
    chosen = lax.dynamic_slice_in_dim(
        mixing.reshape(pairs_n, occupied, occupied), col * second_count, second_count, axis=2
    )
    chosen = chosen.transpose(0, 2, 1).reshape(pairs_n, second_count * occupied)
    hole = lax.dot_general(chosen, placed, (((0,), (0,)), ((), ())), precision=high)
    raw = raw + hole.reshape(raw.shape)
    raw = raw.reshape(second_count, rows_n, first_count, a_count * virtual)
    raw = raw.transpose(1, 2, 0, 3)
    raw = lax.all_to_all(raw, "row", split_axis=0, concat_axis=0, tiled=True)
    raw = raw.transpose(1, 2, 0, 3).reshape(first_count, second_count, virtual * virtual)

    return finish(raw, amplitudes, fock_vir, eps_occ, eps_vir)


F32 = jnp.float32
BF16 = jnp.bfloat16


def split(x):
    high = x.astype(BF16)
    return high, (x - high.astype(F32)).astype(BF16)


def product(a, b, dims):
    return lax.dot_general(a, b, (dims, ((), ())), preferred_element_type=F32)


def contract_kernel(take, slots, flip, v_ref, t_ref, o_ref, buf, rest, spread, high, low, acc, w_high, w_low, sem):
    a_count, b_count, c_count, virtual = v_ref.shape
    group = buf.shape[4 - 1]
    lanes = buf.shape[4]
    tail = virtual - lanes
    rows = take * b_count
    chunks = c_count // group
    blocks = a_count // take
    steps = chunks * blocks
    per = lanes // tail
    width = t_ref.shape[-1]

    def copies(step):
        slot = lax.rem(step, slots)
        chunk, block = step // blocks, lax.rem(step, blocks)
        source = v_ref.at[
            pl.ds(block * take, take), :, pl.ds(pl.multiple_of(chunk * group, group), group), :
        ]
        return (
            pltpu.make_async_copy(source.at[:, :, :, pl.ds(0, lanes)], buf.at[slot], sem.at[slot, 0]),
            pltpu.make_async_copy(source.at[:, :, :, pl.ds(lanes, tail)], rest.at[slot], sem.at[slot, 1]),
        )

    for step in range(min(slots - 1, steps)):
        for copy in copies(step):
            copy.start()
    acc[...] = jnp.zeros_like(acc)
    lane = lax.broadcasted_iota(jnp.int32, (rows, lanes), 1)

    def body(step, _):
        slot = lax.rem(step, slots)
        chunk, block = step // blocks, lax.rem(step, blocks)
        for copy in copies(step):
            copy.wait()

        @pl.when(step + slots - 1 < steps)
        def _():
            for copy in copies(step + slots - 1):
                copy.start()

        @pl.when(block == 0)
        def _():
            for r in range(t_ref.shape[0]):
                for q in range(t_ref.shape[1]):
                    n = t_ref.shape[3]
                    at = (r * t_ref.shape[1] + q) * n
                    hi, lo = split(t_ref[r, q, chunk])
                    w_high[at : at + n, :] = hi
                    w_low[at : at + n, :] = lo

        main = buf.at[slot].reshape(rows * group, lanes)
        spread[:, pl.ds(0, tail)] = rest.at[slot].reshape(rows * group, tail)[...]
        packed = None
        for c in range(group):
            hi, lo = split(main[pl.ds(c, rows, stride=group), :])
            high[:, c * lanes : (c + 1) * lanes] = hi
            low[:, c * lanes : (c + 1) * lanes] = lo
            piece = spread[pl.ds(c, rows, stride=group), :]
            k = c % per
            packed = piece if k == 0 else jnp.where(lane < tail * k, packed, pltpu.roll(piece, tail * k, 1))
            if k == per - 1:
                at = (group + c // per) * lanes
                hi, lo = split(packed)
                high[:, at : at + lanes] = hi
                low[:, at : at + lanes] = lo
        dims = ((1,), (1,))
        acc[block] += (
            product(high[...], w_high[...], dims)
            + product(low[...], w_high[...], dims)
            + product(high[...], w_low[...], dims)
        )
        return 0

    lax.fori_loop(0, steps, body, 0)
    if not flip:
        o_ref[...] = acc[0]
        return
    rows_n, cols_n, _, n, _ = t_ref.shape
    for block in range(blocks):
        turned = acc[block].T
        for r in range(rows_n):
            for q in range(cols_n):
                at = (r * cols_n + q) * n
                o_ref[q, r * n : (r + 1) * n, block * rows : (block + 1) * rows] = turned[at : at + n, :]


def contract(v, t, take, slots, flip):
    a_count, b_count, c_count, virtual = v.shape
    rows_n, cols_n, chunks, n, width = t.shape
    pairs = rows_n * cols_n * n
    group, lanes = c_count // chunks, 128
    rows = take * b_count
    shape = (cols_n, rows_n * n, a_count * b_count) if flip else (rows, pairs)
    return pl.pallas_call(
        functools.partial(contract_kernel, take, slots, flip),
        out_shape=jax.ShapeDtypeStruct(shape, F32),
        in_specs=[pl.BlockSpec(memory_space=pl.ANY), pl.BlockSpec(memory_space=pltpu.VMEM)],
        out_specs=pl.BlockSpec(memory_space=pltpu.VMEM),
        scratch_shapes=[
            pltpu.VMEM((slots, take, b_count, group, lanes), F32),
            pltpu.VMEM((slots, take, b_count, group, virtual - lanes), F32),
            pltpu.VMEM((rows * group, lanes), F32),
            pltpu.VMEM((rows, width), BF16),
            pltpu.VMEM((rows, width), BF16),
            pltpu.VMEM((a_count // take, rows, pairs), F32),
            pltpu.VMEM((pairs, width), BF16),
            pltpu.VMEM((pairs, width), BF16),
            pltpu.SemaphoreType.DMA((slots, 2)),
        ],
        compiler_params=pltpu.CompilerParams(vmem_limit_bytes=60 << 20),
        cost_estimate=pl.CostEstimate(
            flops=6 * v.size * pairs, bytes_accessed=4 * v.size, transcendentals=0
        ),
    )(v, t)


def fast(amplitudes, vvvv, hole_ints, exchange_ints, fock_occ, fock_vir, eps_occ, eps_vir):
    high = lax.Precision.HIGH
    rows_n = lax.axis_size("row")
    cols_n = lax.axis_size("col")
    row = lax.axis_index("row")
    col = lax.axis_index("col")
    first, second, virtual = amplitudes.shape[:3]
    occupied = fock_occ.shape[0]
    pairs = occupied * occupied
    a_count, c_count = vvvv.shape[0], vvvv.shape[2]
    group, lanes = 8, 128
    tail = virtual - lanes
    chunks = c_count // group
    n = first * second

    x = amplitudes.reshape(n, cols_n, chunks, group, virtual)
    x = jnp.concatenate(
        [
            x[..., :lanes].reshape(n, cols_n, chunks, group * lanes),
            x[..., lanes:].reshape(n, cols_n, chunks, group * tail),
        ],
        axis=-1,
    ).transpose(1, 2, 0, 3)
    x = lax.all_to_all(x, "col", split_axis=0, concat_axis=0, tiled=True)
    t = lax.all_gather(x, "row", axis=0)

    chi_part = contract(exchange_ints, t, exchange_ints.shape[0], 3, False)
    chi_all = lax.all_gather(chi_part, ("row", "col"), axis=0)
    chi = chi_all.reshape(rows_n, cols_n, -1, pairs).sum(axis=1).reshape(pairs, pairs)
    delta = jnp.eye(occupied, dtype=fock_occ.dtype)
    known = hole_ints - delta[:, None, :, None] * fock_occ[None, :, None, :]
    known = known.reshape(pairs, rows_n, first, cols_n, second).transpose(0, 3, 1, 2, 4)

    part = contract(vvvv, t, 4, 3, True)

    chi = chi.reshape(pairs, rows_n, cols_n, first, second).transpose(0, 2, 1, 3, 4)
    mixing = (chi + known).reshape(occupied, occupied, pairs)
    wide = t.reshape(rows_n, cols_n, chunks, n, -1)
    main = wide[..., : group * lanes].reshape(rows_n, cols_n, chunks, n, group, lanes)
    rest = wide[..., group * lanes :].reshape(rows_n, cols_n, chunks, n, group, tail)
    whole = jnp.concatenate([main, rest], axis=-1)
    mine = lax.dynamic_slice_in_dim(whole, row * a_count, a_count, axis=5)
    mine = mine.reshape(rows_n, cols_n, chunks, first, second, group, a_count)
    mine = mine.transpose(1, 4, 0, 3, 6, 2, 5).reshape(pairs, a_count * c_count)
    hole = lax.dot_general(
        mixing.reshape(pairs, pairs), mine, (((0,), (0,)), ((), ())), precision=high
    )
    hole = hole.reshape(cols_n, rows_n * n, a_count, c_count)
    part = part.reshape(cols_n, rows_n * n, a_count, virtual)
    spot = lax.dynamic_slice_in_dim(part, col * c_count, c_count, axis=3) + hole
    part = lax.dynamic_update_slice_in_dim(part, spot, col * c_count, axis=3)
    part = part.reshape(cols_n, rows_n * n, a_count * virtual)
    raw = lax.psum_scatter(part, "col", scatter_dimension=0, tiled=False)
    raw = raw.reshape(rows_n, n, a_count * virtual)
    raw = lax.all_to_all(raw, "row", split_axis=0, concat_axis=0, tiled=True)
    raw = raw.transpose(1, 0, 2).reshape(first, second, virtual * virtual)
    return finish(raw, amplitudes, fock_vir, eps_occ, eps_vir)


def on_device(amplitudes, vvvv, *rest):
    virtual, b_count, c_count = amplitudes.shape[2], vvvv.shape[1], vvvv.shape[2]
    tail = virtual - 128
    fits = (
        virtual > 128
        and 128 % tail == 0
        and c_count % 8 == 0
        and (8 * tail) % 128 == 0
        and vvvv.shape[0] % 4 == 0
        and (4 * b_count) % 128 == 0
        and (amplitudes.shape[0] * amplitudes.shape[1]) % 8 == 0
    )
    return (fast if fits else plain)(amplitudes, vvvv, *rest)


def solution(mesh):
    in_specs = (
        P("row", "col", None, None),
        P("row", None, "col", None),
        P(),
        P("row", None, "col", None),
        P(),
        P(),
        P(),
        P(),
    )
    out_specs = P("row", "col", None, None)
    return jax.shard_map(
        on_device, mesh=mesh, in_specs=in_specs, out_specs=out_specs, check_vma=False
    )
```

time: 434 us -> 450 us (1.037)
  matrix products: 142 us -> 6.33 us
  Pallas kernels: 0 us -> 79.5 us
  local copies, waits for them, and re-layouts: 70.2 us -> 135 us
  other arithmetic: 2.17 us -> 13 us
  blocking collectives: 18.8 us -> 13.4 us
    dot_general x5 -> x3, matrix products: 142 us -> 6.33 us  [the longest x1 2.4 us: finish(): jnp.einsum('ijac,cb->ijab', amplitudes, fock_vir, precision=high)]
    pallas_call x0 -> x2, Pallas kernels: none -> 79.5 us  [contract(): pl.pallas_call(functools.partial(contract_kernel, take, slots, flip), out...]
    dynamic_update_slice x0 -> x1, local copies, waits for them, and re-layouts: none -> 54.8 us  [fast(): part = lax.dynamic_update_slice_in_dim(part, spot, col * c_count, axis=3)]
    unnamed x4, waiting for transfers between devices: 0.07 us -> 43.3 us
    reduce_scatter x1 -> x0, waiting for transfers between devices: 35.2 us -> none  [on_device(): raw = lax.psum_scatter(part, 'col', scatter_dimension=0, tiled=True)]
    reshape x7 -> x11, local copies, waits for them, and re-layouts: 22.4 us -> 39.2 us  [the longest x1 11 us: fast(): mine = mine.transpose(1, 4, 0, 3, 6, 2, 5).reshape(pairs, a_count * c_count)]
    concatenate x0 -> x1, other arithmetic: none -> 9.13 us  [fast(): whole = jnp.concatenate([main, rest], axis=-1)]
    all_gather x1 -> x0, local copies, waits for them, and re-layouts: 8.17 us -> none  [on_device(): gathered = lax.all_gather(split, 'row', axis=0, tiled=True)]
  transfers between devices with their start and end apart: 7 -> 6, of which waited for: 5 -> 5; matrix products, arithmetic and copies ran while one was open for 42% -> 5% of each run, Pallas kernels for 0% -> 16%
where the time goes in v1:
time: 450 us; the launch traced here: 448 us
  waiting for transfers between devices  176 us (39%)
  local copies, waits for them, and re-layouts  135 us (30%)
  Pallas kernels  79.5 us (18%)
  blocking collectives  13.4 us (3%)
  between operations  13.4 us (3%)
  other arithmetic  13 us (3%)
  starting transfers between devices  11.4 us (3%)
  matrix products  6.33 us (1%)
    pallas_call x2, Pallas kernels, contract(): pl.pallas_call(functools.partial(contract_kernel, take, slots, flip), out...  79.5 us
    all_gather x1, waiting for transfers between devices, fast(): t = lax.all_gather(x, 'row', axis=0)  61.9 us
    dynamic_update_slice x1, local copies, waits for them, and re-layouts, fast(): part = lax.dynamic_update_slice_in_dim(part, spot, col * c_count, axis=3)  54.8 us
    ppermute x2, waiting for transfers between devices, finish(): others.append(lax.ppermute(block, ('row', 'col'), route))  50.4 us
    unnamed x4, waiting for transfers between devices  43.3 us
    all_to_all x1, waiting for transfers between devices, fast(): raw = lax.all_to_all(raw, 'row', split_axis=0, concat_axis=0, tiled=True)  20.4 us
    transpose x1, local copies, waits for them, and re-layouts, fast(): mine = mine.transpose(1, 4, 0, 3, 6, 2, 5).reshape(pairs, a_count * c_count)  17.8 us
    all_to_all x1, blocking collectives, fast(): x = lax.all_to_all(x, 'col', split_axis=0, concat_axis=0, tiled=True)  13.4 us
  transfers between devices with their start and end apart: 6, of which 5 were waited for; matrix products, arithmetic and copies ran while one was open for 5% of the time, Pallas kernels for 16%

profile of v1, /device:TPU:3, one launch (start us, length us, event | category | flops | bytes accessed | tf_op | source)
XLA Modules:
  0.0 448.4 jit_solution(7802549718621573816)
XLA Ops:
  9.7 13.4 %all_to_all.10 = f32[4,5,8,1280]{3,2,1,0:T(8,128)} all-to-all(f32[4,5,8,1280]{3,2,1,0:T(8,128)S(1)} %maximum_bitcast_fusion), channel_id=1, replica_groups=mesh['row'=8,'col'=4] {'col'}, dimensions={0} | all-to-all | bytes 1638400 | tf_op jit(solution)/shard_map/all_to_all | solution.py:250
  27.1 3.1 reshape.184
  30.2 61.9 %all-gather.5.cloned.1.call-done = f32[32,5,8,1280]{3,2,1,0:T(8,128)} async-done(((f32[4,5,8,1280]{3,2,1,0:T(8,128)}), f32[32,5,8,1280]{3,2,1,0:T(8,128)}) %all-gather.5.cloned.1.call-update) | async-done | bytes 6553616 | tf_op jit(solution)/shard_map/all_gather | solution.py:251
  92.1 3.1 slice_bitcast_fusion
  96.7 3.6 copy.52
  100.3 2.9 reshape.186
  103.2 9.1 %fusion = f32[8,4,5,8,8,20]{5,4,3,2,1,0:T(8,128)} fusion(s32[]{:T(128)S(6)} %select_n.30, f32[8,4,5,8,8,128]{5,4,3,2,1,0:T(8,128)} %copy.52, f32[8,4,5,8,8,32]{5,4,3,2,1,0:T(8,128)} %reshape.186), kind=kLoop, calls=%fused_computation.3 | loop fusion | flops 204800 | bytes 7372804 | tf_op jit(solution)/shard_map/concatenate | solution.py:267
  112.3 17.8 %copy.53 = f32[4,4,8,2,20,5,8]{6,5,4,3,2,1,0:T(8,128)} copy(f32[4,4,8,2,20,5,8]{4,6,1,3,5,0,2:T(8,128)} %bitcast.72) | data formatting | bytes 1638400 | tf_op jit(solution)/shard_map/transpose | solution.py:270
  130.2 11.0 %reshape.188 = f32[256,800]{1,0:T(8,128)S(1)} reshape(f32[4,4,8,2,20,5,8]{6,5,4,3,2,1,0:T(8,128)} %copy.53) | data formatting | bytes 1638400 | tf_op jit(solution)/shard_map/reshape | solution.py:270
  142.4 8.3 %shard_map.83 = f32[32,256]{1,0:T(8,128)} custom-call(f32[2,16,40,160]{3,2,1,0:T(8,128)} %v_ref.3, f32[8,4,5,8,1280]{4,3,2,1,0:T(8,128)} %bitcast.70), custom_call_target="tpu_custom_call" | custom-call | flops 314572800 | bytes 819200 | tf_op jit(solution)/shard_map/pallas_call | solution.py:204
  150.9 71.3 %shard_map.82 = f32[4,64,3200]{2,1,0:T(8,128)} custom-call(f32[20,160,40,160]{3,2,1,0:T(8,128)} %v_ref.2, f32[8,4,5,8,1280]{4,3,2,1,0:T(8,128)} %bitcast.71), custom_call_target="tpu_custom_call" | custom-call | flops 31457280000 | bytes 81920000 | tf_op jit(solution)/shard_map/pallas_call | solution.py:204
  222.2 6.4 %reshape.182 = f32[4,64,20,160]{3,2,1,0:T(8,128)} reshape(f32[4,64,3200]{2,1,0:T(8,128)} %shard_map.82) | data formatting | bytes 6553600 | tf_op jit(solution)/shard_map/reshape | solution.py:275
  228.7 3.7 constant_dynamic-slice_fusion.2
  239.7 2.2 copy.55
  241.9 54.8 %dynamic_update_slice.3 = f32[4,64,20,160]{3,2,1,0:T(8,128)} dynamic-update-slice(f32[4,64,20,160]{3,2,1,0:T(8,128)} %reshape.182, f32[4,64,20,40]{3,2,1,0:T(8,128)S(1)} %copy.55, s32[]{:T(128)} %constant.13.clone.1, s32[]{:T(128)} %constant.13.clone.1, s32[]{:T(128)} %constant.13.clone.1, s32[]{:T(128)S(6)} %select_n.29) | dynamic-update-slice | bytes 1638404 | tf_op jit(solution)/shard_map/dynamic_update_slice | solution.py:277
  296.7 6.1 %reshape.189 = f32[4,64,3200]{2,1,0:T(8,128)} reshape(f32[4,64,20,160]{3,2,1,0:T(8,128)} %dynamic_update_slice.3) | data formatting | bytes 6553600 | tf_op jit(solution)/shard_map/reshape | solution.py:278
  302.9 43.2 %reduce-scatter.4.cloned.1.call-done = f32[1,64,3200]{2,1,0:T(8,128)} async-done(((f32[4,64,3200]{2,1,0:T(8,128)}), f32[1,64,3200]{2,1,0:T(8,128)}) %reduce-scatter.4.cloned.1.call-update) | async-done | bytes 819216
  346.1 5.4 %all-to-all-start.1 = ((f32[8,8,3200]{2,1,0:T(8,128)}), f32[8,8,3200]{2,1,0:T(8,128)S(1)}, u32[]{:S(2)}, u32[]{:S(2)}) async-start(f32[8,8,3200]{2,1,0:T(8,128)} %bitcast.83), calls=%async_computation.1 | async-start | bytes 1638400 | tf_op jit(solution)/shard_map/all_to_all | solution.py:281
  351.8 20.4 %all-to-all-done.1 = f32[8,8,3200]{2,1,0:T(8,128)S(1)} async-done(((f32[8,8,3200]{2,1,0:T(8,128)}), f32[8,8,3200]{2,1,0:T(8,128)S(1)}, u32[]{:S(2)}, u32[]{:S(2)}) %all-to-all-start.1) | async-done | bytes 819232 | tf_op jit(solution)/shard_map/all_to_all | solution.py:281
  375.2 3.6 collective-permute-start.1
  380.6 40.9 %collective-permute-done = f32[2,2,25600]{2,1,0:T(2,128)S(1)} collective-permute-done((f32[2,2,25600]{2,1,0:T(2,128)S(1)}, f32[2,2,25600]{2,1,0:T(2,128)S(1)}, u32[]{:S(2)}, u32[]{:S(2)}) %collective-permute-start) | collective-permute-done | bytes 409632 | tf_op jit(solution)/shard_map/ppermute | solution.py:27
  421.5 9.5 %collective-permute-done.1 = f32[2,2,25600]{2,1,0:T(2,128)S(1)} collective-permute-done((f32[2,2,25600]{2,1,0:T(2,128)S(1)}, f32[2,2,25600]{2,1,0:T(2,128)S(1)}, u32[]{:S(2)}, u32[]{:S(2)}) %collective-permute-start.1) | collective-permute-done | bytes 409632 | tf_op jit(solution)/shard_map/ppermute | solution.py:27
  431.3 2.3 gather_fusion
  437.5 2.4 convolution_add_fusion.1
  (57 shorter events, 28.4 us)
Async XLA Ops:
  6.5 430.9 %copy-start = (f32[160,160]{1,0:T(8,128)S(1)}, f32[160,160]{1,0:T(8,128)}, u32[]{:S(2)}) copy-start(f32[160,160]{1,0:T(8,128)} %param.13) | copy-start | bytes 307204
  6.5 85.6 %all-gather.5.cloned.1.call-start = ((), (), s32[]{:S(2)}) async-start(), calls=%async_computation.3 | async-start | bytes 7372800 | tf_op jit(solution)/shard_map/all_gather | solution.py:251
  9.6 13.6 %copy-start.5 = (f32[16,16]{1,0:T(8,128)S(1)}, f32[16,16]{1,0:T(8,128)}, u32[]{:S(2)}) copy-start(f32[16,16]{1,0:T(8,128)} %param.12) | copy-start | bytes 3076
  23.1 211.1 %all-gather.7.cloned.1.call-start = ((), (), s32[]{:S(2)}) async-start(), calls=%async_computation.4 | async-start | bytes 1081344 | tf_op jit(solution)/shard_map/all_gather | solution.py:254
  150.7 195.4 %reduce-scatter.4.cloned.1.call-start = ((), (), s32[]{:S(2)}) async-start(), calls=%async_computation.5 | async-start | bytes 4096000
  234.2 2.2 copy-start.4
  235.6 1.4 copy-start.1
  236.4 1.3 copy-start.3
  302.8 48.7 %copy-start.7 = (f32[16]{0:T(128)S(1)}, f32[16]{0:T(128)}, u32[]{:S(2)}) copy-start(f32[16]{0:T(128)} %param.14) | copy-start | bytes 196
  346.1 26.1 %all-to-all-start.1 = ((f32[8,8,3200]{2,1,0:T(8,128)}), f32[8,8,3200]{2,1,0:T(8,128)S(1)}, u32[]{:S(2)}, u32[]{:S(2)}) async-start(f32[8,8,3200]{2,1,0:T(8,128)} %bitcast.83), calls=%async_computation.1 | async-start | bytes 1638400 | tf_op jit(solution)/shard_map/all_to_all | solution.py:281
  372.2 6.7 %copy-start.6 = (f32[160]{0:T(256)S(1)}, f32[160]{0:T(256)}, u32[]{:S(2)}) copy-start(f32[160]{0:T(256)} %param.15) | copy-start | bytes 1924
  373.1 48.4 %collective-permute-start = (f32[2,2,25600]{2,1,0:T(2,128)S(1)}, f32[2,2,25600]{2,1,0:T(2,128)S(1)}, u32[]{:S(2)}, u32[]{:S(2)}) collective-permute-start(f32[2,2,25600]{2,1,0:T(2,128)S(1)} %get-tuple-element.5), channel_id=1, source_target_pairs={{0,0},{1,8},{2,16},{3,24},{4,4},{5,12},{6,20},{7,28},{8,1},{9,9},{... | collective-permute-start | bytes 1228808 | tf_op jit(solution)/shard_map/ppermute | solution.py:27
  375.2 55.7 %collective-permute-start.1 = (f32[2,2,25600]{2,1,0:T(2,128)S(1)}, f32[2,2,25600]{2,1,0:T(2,128)S(1)}, u32[]{:S(2)}, u32[]{:S(2)}) collective-permute-start(f32[2,2,25600]{2,1,0:T(2,128)S(1)} %get-tuple-element.6), channel_id=1, source_target_pairs={{0,4},{1,12},{2,20},{3,28},{4,0},{5,8},{6,16},{7,24},{8,5},{9,13},... | collective-permute-start | bytes 1228808 | tf_op jit(solution)/shard_map/ppermute | solution.py:27
  433.6 3.9 copy-start.2
Sparse Core Ops, SparseCore 0:
  23.2 68.8 all-gather.4
  150.8 52.1 all-gather.6
  303.0 43.0 reduce-scatter.3

commit v2 on v1

--- a/solution.py
+++ b/solution.py
@@ -31,6 +31,14 @@
     other = other.transpose(2, 0, 1, 4, 3)
     other = other.reshape(first_count, second_count, virtual, virtual)
     total = raw.reshape(first_count, second_count, virtual, virtual) + other
+    return close(total, amplitudes, fock_vir, eps_occ, eps_vir)
+
+
+def close(total, amplitudes, fock_vir, eps_occ, eps_vir):
+    high = lax.Precision.HIGH
+    row = lax.axis_index("row")
+    col = lax.axis_index("col")
+    first_count, second_count = amplitudes.shape[:2]
     total = total + jnp.einsum("ijac,cb->ijab", amplitudes, fock_vir, precision=high)
     total = total + jnp.einsum("ac,ijcb->ijab", fock_vir, amplitudes, precision=high)
     energy_rows = lax.dynamic_slice_in_dim(eps_occ, row * first_count, first_count)
@@ -108,7 +116,7 @@
     return lax.dot_general(a, b, (dims, ((), ())), preferred_element_type=F32)
 
 
-def contract_kernel(take, slots, flip, v_ref, t_ref, o_ref, buf, rest, spread, high, low, acc, w_high, w_low, sem):
+def contract_kernel(take, slots, v_ref, t_ref, o_ref, buf, rest, spread, high, low, acc, w_high, w_low, sem):
     a_count, b_count, c_count, virtual = v_ref.shape
     group = buf.shape[4 - 1]
     lanes = buf.shape[4]
@@ -151,10 +159,10 @@
         @pl.when(block == 0)
         def _():
             for r in range(t_ref.shape[0]):
-                for q in range(t_ref.shape[1]):
+                for q in range(t_ref.shape[2]):
                     n = t_ref.shape[3]
-                    at = (r * t_ref.shape[1] + q) * n
-                    hi, lo = split(t_ref[r, q, chunk])
+                    at = (r * t_ref.shape[2] + q) * n
+                    hi, lo = split(t_ref[r, chunk, q])
                     w_high[at : at + n, :] = hi
                     w_low[at : at + n, :] = lo
 
@@ -182,27 +190,19 @@
         return 0
 
     lax.fori_loop(0, steps, body, 0)
-    if not flip:
-        o_ref[...] = acc[0]
-        return
-    rows_n, cols_n, _, n, _ = t_ref.shape
     for block in range(blocks):
-        turned = acc[block].T
-        for r in range(rows_n):
-            for q in range(cols_n):
-                at = (r * cols_n + q) * n
-                o_ref[q, r * n : (r + 1) * n, block * rows : (block + 1) * rows] = turned[at : at + n, :]
-
-
-def contract(v, t, take, slots, flip):
+        o_ref[block * rows : (block + 1) * rows, :] = acc[block]
+
+
+def contract(v, t, take, slots):
     a_count, b_count, c_count, virtual = v.shape
-    rows_n, cols_n, chunks, n, width = t.shape
+    rows_n, chunks, cols_n, n, width = t.shape
     pairs = rows_n * cols_n * n
     group, lanes = c_count // chunks, 128
     rows = take * b_count
-    shape = (cols_n, rows_n * n, a_count * b_count) if flip else (rows, pairs)
+    shape = (a_count * b_count, pairs)
     return pl.pallas_call(
-        functools.partial(contract_kernel, take, slots, flip),
+        functools.partial(contract_kernel, take, slots),
         out_shape=jax.ShapeDtypeStruct(shape, F32),
         in_specs=[pl.BlockSpec(memory_space=pl.ANY), pl.BlockSpec(memory_space=pltpu.VMEM)],
         out_specs=pl.BlockSpec(memory_space=pltpu.VMEM),
@@ -224,6 +224,263 @@
     )(v, t)
 
 
+def hole_kernel(a_count, c_count, virtual, part_ref, t_ref, mixing_ref, o_ref, w_high, w_low, picked, add):
+    rows_n, chunks, cols_n, n, width = t_ref.shape
+    pairs = rows_n * cols_n * n
+    lanes = 128
+    tail = virtual - lanes
+    group = c_count // chunks
+    per = lanes // tail
+    b_count = part_ref.shape[0] // a_count
+    row, col = lax.axis_index("row"), lax.axis_index("col")
+    up = -(-a_count // 16) * 16
+    spot = row * a_count + lax.broadcasted_iota(jnp.int32, (up, lanes), 0)
+    lane = lax.broadcasted_iota(jnp.int32, (up, lanes), 1)
+    first = jnp.where(spot == lane, 1.0, 0.0).astype(BF16)
+    later = [jnp.where(spot - lanes == lane - k * tail, 1.0, 0.0) for k in range(per)]
+    later = [
+        jnp.where((lane >= k * tail) & (lane < (k + 1) * tail), later[k], 0.0).astype(BF16)
+        for k in range(per)
+    ]
+    dims = ((1,), (1,))
+    for chunk in range(chunks):
+        for r in range(rows_n):
+            for q in range(cols_n):
+                at = (r * cols_n + q) * n
+                hi, lo = split(t_ref[r, chunk, q])
+                w_high[at : at + n, :] = hi
+                w_low[at : at + n, :] = lo
+        for c in range(group):
+            at = (group + c // per) * lanes
+            k = c % per
+            total = None
+            for w in (w_high, w_low):
+                value = product(first, w[:, c * lanes : (c + 1) * lanes], dims)
+                value += product(later[k], w[:, at : at + lanes], dims)
+                total = value if total is None else total + value
+            for half in range(pairs // lanes):
+                picked[half, pl.ds(chunk * group + c, a_count, stride=c_count), :] = total[
+                    :a_count, half * lanes : (half + 1) * lanes
+                ]
+    mix_high, mix_low = split(mixing_ref[...])
+    total = None
+    for half in range(pairs // lanes):
+        hi, lo = split(picked[half])
+        at = slice(half * lanes, (half + 1) * lanes)
+        value = (
+            product(hi, mix_high[at, :], ((1,), (0,)))
+            + product(lo, mix_high[at, :], ((1,), (0,)))
+            + product(hi, mix_low[at, :], ((1,), (0,)))
+        )
+        total = value if total is None else total + value
+    add[...] = part_ref[...]
+    for a in range(a_count):
+        at = pl.ds(pl.multiple_of(a * b_count + col * c_count, 8), c_count)
+        add[at, :] += total[a * c_count : (a + 1) * c_count, :]
+    step = 5 * lanes
+    for block in range(part_ref.shape[0] // step):
+        turned = add[block * step : (block + 1) * step, :].T
+        for r in range(rows_n):
+            for q in range(cols_n):
+                at = (r * cols_n + q) * n
+                for h in range(2):
+                    o_ref[q, r, h, :, block * step : (block + 1) * step] = turned[
+                        at + h * n // 2 : at + (h + 1) * n // 2, :
+                    ]
+
+
+def hole(part, t, mixing, a_count, c_count, virtual):
+    rows_n, chunks, cols_n, n, width = t.shape
+    pairs = rows_n * cols_n * n
+    return pl.pallas_call(
+        functools.partial(hole_kernel, a_count, c_count, virtual),
+        out_shape=jax.ShapeDtypeStruct((cols_n, rows_n, 2, n // 2, part.shape[0]), F32),
+        in_specs=[pl.BlockSpec(memory_space=pltpu.VMEM)] * 3,
+        out_specs=pl.BlockSpec(memory_space=pltpu.VMEM),
+        scratch_shapes=[
+            pltpu.VMEM((pairs, width), BF16),
+            pltpu.VMEM((pairs, width), BF16),
+            pltpu.VMEM((pairs // 128, a_count * c_count, 128), F32),
+            pltpu.VMEM(part.shape, F32),
+        ],
+        compiler_params=pltpu.CompilerParams(vmem_limit_bytes=60 << 20),
+    )(part, t, mixing)
+
+
+def exchange_kernel(
+    part_ref, straight_ref, turned_ref, got, last, onward, sums, middle,
+    send_a, recv_a, send_b, recv_b, send_c, recv_c, send_d, recv_d, send_e, recv_e, own,
+):
+    cols_n, rows_n = part_ref.shape[:2]
+    row, col = lax.axis_index("row"), lax.axis_index("col")
+    flips = (col + 1 - 2 * (col % 2), (col + 2) % 4)
+    far = 3 - col
+
+    def remote(source, target, send, recv, r, q):
+        return pltpu.make_async_remote_copy(
+            src_ref=source, dst_ref=target, send_sem=send, recv_sem=recv,
+            device_id=(r, q), device_id_type=pl.DeviceIdType.MESH,
+        )
+
+    barrier = pltpu.get_barrier_semaphore()
+    for q in (flips[0], flips[1], far):
+        pl.semaphore_signal(barrier, inc=1, device_id=(row, q), device_id_type=pl.DeviceIdType.MESH)
+    for k in range(1, rows_n):
+        r = (row + k) % rows_n
+        pl.semaphore_signal(barrier, inc=1, device_id=(r, col), device_id_type=pl.DeviceIdType.MESH)
+    pl.semaphore_wait(barrier, cols_n - 1 + rows_n - 1)
+
+    def pair(k):
+        return flips if k < rows_n // 2 else (flips[1], flips[0])
+
+    def scatter(k):
+        near = pair(k)[0]
+        return [
+            remote(part_ref.at[near, k], got.at[k, 0], send_a.at[k, 0], recv_a.at[k, 0], row, near),
+            remote(part_ref.at[far, k], got.at[k, 1], send_a.at[k, 1], recv_a.at[k, 1], row, near),
+        ]
+
+    def pass_on(k):
+        return remote(onward.at[k], last.at[k], send_b.at[k], recv_b.at[k], row, pair(k)[1])
+
+    def deliver(k):
+        return remote(sums.at[k], straight_ref.at[row], send_c.at[k], recv_c.at[row], k, col)
+
+    def deliver_own(k):
+        return pltpu.make_async_copy(sums.at[k], straight_ref.at[row], own.at[0])
+
+    def cross(k):
+        return remote(sums.at[k], middle.at[k % 2, col], send_d.at[k], recv_d.at[k % 2, col], row, k // 2)
+
+    def cross_own(k):
+        return pltpu.make_async_copy(sums.at[k], middle.at[k % 2, col], own.at[1 + k % 2])
+
+    def spread(m, q, h):
+        return remote(
+            middle.at[m, q, h], turned_ref.at[row, m], send_e.at[m, q, h], recv_e.at[row, m], 2 * q + h, col
+        )
+
+    def spread_own(m, q, h):
+        return pltpu.make_async_copy(middle.at[m, q, h], turned_ref.at[row, m], own.at[3 + m])
+
+    order = [k for m in range(rows_n // 2) for k in (m, rows_n // 2 + m)]
+    ahead = 4
+    for k in order[:ahead]:
+        for copy in scatter(k):
+            copy.start()
+
+    def first(k):
+        for copy in scatter(k):
+            copy.wait_recv()
+        onward[k] = part_ref[pair(k)[1], k] + got[k, 1]
+        sums[k] = part_ref[col, k] + got[k, 0]
+        pass_on(k).start()
+
+    def second(k):
+        pass_on(k).wait_recv()
+        sums[k] = sums[k] + last[k]
+
+        @pl.when(row != k)
+        def _():
+            deliver(k).start()
+
+        @pl.when(row == k)
+        def _():
+            deliver_own(k).start()
+
+        @pl.when(col != k // 2)
+        def _():
+            cross(k).start()
+
+        @pl.when(col == k // 2)
+        def _():
+            cross_own(k).start()
+
+    for at, k in enumerate(order):
+        if at + ahead < rows_n:
+            for copy in scatter(order[at + ahead]):
+                copy.start()
+        first(k)
+        if at >= 2:
+            second(order[at - 2])
+    for k in order[-2:]:
+        second(k)
+
+    def arrived(m, q):
+        @pl.when(col != q)
+        def _():
+            remote(sums.at[0], middle.at[m, q], send_d.at[0], recv_d.at[m, q], row, q).wait_recv()
+
+    for m in range(2):
+        for k in range(cols_n):
+            @pl.when(col == k)
+            def _():
+                cross_own(2 * k + m).wait()
+    for m in range(2):
+        for q in range(cols_n):
+            arrived(m, q)
+            for h in range(2):
+                @pl.when(row != 2 * q + h)
+                def _():
+                    spread(m, q, h).start()
+
+                @pl.when(row == 2 * q + h)
+                def _():
+                    spread_own(m, q, h).start()
+    for k in range(rows_n):
+        for copy in scatter(k):
+            copy.wait_send()
+        pass_on(k).wait_send()
+
+        @pl.when(row != k)
+        def _():
+            deliver(k).wait_send()
+            remote(sums.at[0], straight_ref.at[k], send_c.at[k], recv_c.at[k], k, col).wait_recv()
+            for m in range(2):
+                spread(m, k // 2, k % 2).wait_send()
+                remote(
+                    middle.at[m, 0, 0], turned_ref.at[k, m], send_e.at[m, 0, 0], recv_e.at[k, m], k, col
+                ).wait_recv()
+
+        @pl.when(row == k)
+        def _():
+            deliver_own(k).wait()
+            for m in range(2):
+                spread_own(m, k // 2, k % 2).wait()
+
+        @pl.when(col != k // 2)
+        def _():
+            cross(k).wait_send()
+
+
+def exchange(part):
+    cols_n, rows_n, _, n, width = part.shape
+    block = (2, n, width)
+    dma = pltpu.SemaphoreType.DMA
+    return pl.pallas_call(
+        exchange_kernel,
+        out_shape=[jax.ShapeDtypeStruct((rows_n,) + block, F32)] * 2,
+        in_specs=[pl.BlockSpec(memory_space=pltpu.VMEM)],
+        out_specs=[pl.BlockSpec(memory_space=pltpu.VMEM)] * 2,
+        scratch_shapes=[
+            pltpu.VMEM((rows_n, 2) + block, F32),
+            pltpu.VMEM((rows_n,) + block, F32),
+            pltpu.VMEM((rows_n,) + block, F32),
+            pltpu.VMEM((rows_n,) + block, F32),
+            pltpu.VMEM((2, cols_n) + block, F32),
+            dma((rows_n, 2)), dma((rows_n, 2)),
+            dma((rows_n,)), dma((rows_n,)),
+            dma((rows_n,)), dma((rows_n,)),
+            dma((rows_n,)), dma((2, cols_n)),
+            dma((2, cols_n, 2)), dma((rows_n, 2)),
+            dma((5,)),
+        ],
+        compiler_params=pltpu.CompilerParams(
+            collective_id=1, has_side_effects=True, vmem_limit_bytes=40 << 20
+        ),
+    )(part)
+
+
 def fast(amplitudes, vvvv, hole_ints, exchange_ints, fock_occ, fock_vir, eps_occ, eps_vir):
     high = lax.Precision.HIGH
     rows_n = lax.axis_size("row")
@@ -239,7 +496,9 @@
     chunks = c_count // group
     n = first * second
 
-    x = amplitudes.reshape(n, cols_n, chunks, group, virtual)
+    half = second // 2
+    x = amplitudes.reshape(first, 2, half, virtual, virtual).transpose(1, 0, 2, 3, 4)
+    x = x.reshape(n, cols_n, chunks, group, virtual)
     x = jnp.concatenate(
         [
             x[..., :lanes].reshape(n, cols_n, chunks, group * lanes),
@@ -248,39 +507,35 @@
         axis=-1,
     ).transpose(1, 2, 0, 3)
     x = lax.all_to_all(x, "col", split_axis=0, concat_axis=0, tiled=True)
-    t = lax.all_gather(x, "row", axis=0)
-
-    chi_part = contract(exchange_ints, t, exchange_ints.shape[0], 3, False)
+    t = lax.all_gather(x.transpose(1, 0, 2, 3), "row", axis=0)
+
+    chi_part = contract(exchange_ints, t, exchange_ints.shape[0], 3)
     chi_all = lax.all_gather(chi_part, ("row", "col"), axis=0)
     chi = chi_all.reshape(rows_n, cols_n, -1, pairs).sum(axis=1).reshape(pairs, pairs)
     delta = jnp.eye(occupied, dtype=fock_occ.dtype)
     known = hole_ints - delta[:, None, :, None] * fock_occ[None, :, None, :]
-    known = known.reshape(pairs, rows_n, first, cols_n, second).transpose(0, 3, 1, 2, 4)
-
-    part = contract(vvvv, t, 4, 3, True)
-
-    chi = chi.reshape(pairs, rows_n, cols_n, first, second).transpose(0, 2, 1, 3, 4)
-    mixing = (chi + known).reshape(occupied, occupied, pairs)
-    wide = t.reshape(rows_n, cols_n, chunks, n, -1)
-    main = wide[..., : group * lanes].reshape(rows_n, cols_n, chunks, n, group, lanes)
-    rest = wide[..., group * lanes :].reshape(rows_n, cols_n, chunks, n, group, tail)
-    whole = jnp.concatenate([main, rest], axis=-1)
-    mine = lax.dynamic_slice_in_dim(whole, row * a_count, a_count, axis=5)
-    mine = mine.reshape(rows_n, cols_n, chunks, first, second, group, a_count)
-    mine = mine.transpose(1, 4, 0, 3, 6, 2, 5).reshape(pairs, a_count * c_count)
-    hole = lax.dot_general(
-        mixing.reshape(pairs, pairs), mine, (((0,), (0,)), ((), ())), precision=high
-    )
-    hole = hole.reshape(cols_n, rows_n * n, a_count, c_count)
-    part = part.reshape(cols_n, rows_n * n, a_count, virtual)
-    spot = lax.dynamic_slice_in_dim(part, col * c_count, c_count, axis=3) + hole
-    part = lax.dynamic_update_slice_in_dim(part, spot, col * c_count, axis=3)
-    part = part.reshape(cols_n, rows_n * n, a_count * virtual)
-    raw = lax.psum_scatter(part, "col", scatter_dimension=0, tiled=False)
-    raw = raw.reshape(rows_n, n, a_count * virtual)
-    raw = lax.all_to_all(raw, "row", split_axis=0, concat_axis=0, tiled=True)
-    raw = raw.transpose(1, 0, 2).reshape(first, second, virtual * virtual)
-    return finish(raw, amplitudes, fock_vir, eps_occ, eps_vir)
+    highest = lax.Precision.HIGHEST
+    one, two = jnp.divmod(jnp.arange(pairs, dtype=jnp.int32), occupied)
+
+    def place(i, j):
+        inner = (j % second) // half * (first * half) + (i % first) * half + j % half
+        return ((i // first) * cols_n + j // second) * n + inner
+
+    spots = jnp.arange(pairs, dtype=jnp.int32)
+    turn = (place(one, two)[:, None] == spots[None, :]).astype(F32)
+    move = (spots[:, None] == place(two, one)[None, :]).astype(F32)
+    known = jnp.dot(known.reshape(pairs, pairs), turn, precision=highest)
+
+    part = contract(vvvv, t, 4, 3)
+
+    mixing = jnp.dot(move, chi + known, precision=highest)
+    part = hole(part, t, mixing, a_count, c_count, virtual)
+    straight, turned = exchange(part)
+    straight = straight.reshape(rows_n, 2, first, half, a_count, virtual)
+    straight = straight.transpose(2, 1, 3, 0, 4, 5).reshape(first, second, virtual, virtual)
+    turned = turned.reshape(rows_n, 2, half, first, a_count, virtual)
+    turned = turned.transpose(3, 1, 2, 5, 0, 4).reshape(first, second, virtual, virtual)
+    return close(straight + turned, amplitudes, fock_vir, eps_occ, eps_vir)
 
 
 def on_device(amplitudes, vvvv, *rest):
@@ -294,6 +549,9 @@
         and vvvv.shape[0] % 4 == 0
         and (4 * b_count) % 128 == 0
         and (amplitudes.shape[0] * amplitudes.shape[1]) % 8 == 0
+        and amplitudes.shape[1] == 2 * amplitudes.shape[0]
+        and lax.axis_size("row") == 2 * lax.axis_size("col")
+        and lax.axis_size("col") == 4
     )
     return (fast if fits else plain)(amplitudes, vvvv, *rest)
 

time: 450 us -> 275 us (0.61)
  the two profiles are of different devices: /device:TPU:3 before, /device:TPU:1 now
where the time goes in v2:
time: 275 us
  Pallas kernels  152 us (55%)
  waiting for transfers between devices  64.9 us (24%)
  local copies, waits for them, and re-layouts  21.4 us (8%)
  blocking collectives  15.2 us (6%)
  between operations  13.6 us (5%)
  matrix products  3.99 us (1%)
  other arithmetic  3.39 us (1%)
    pallas_call x2, Pallas kernels, contract(): pl.pallas_call(functools.partial(contract_kernel, take, slots), out_shape...  78.8 us
    all_gather x1, waiting for transfers between devices, fast(): t = lax.all_gather(x.transpose(1, 0, 2, 3), 'row', axis=0)  64.9 us
    pallas_call x1, Pallas kernels, exchange(): pl.pallas_call(exchange_kernel, out_shape=[jax.ShapeDtypeStruct((rows_n,)...  62.3 us
    all_to_all x1, blocking collectives, fast(): x = lax.all_to_all(x, 'col', split_axis=0, concat_axis=0, tiled=True)  15.2 us
    pallas_call x1, Pallas kernels, hole(): pl.pallas_call(functools.partial(hole_kernel, a_count, c_count, virtual),...  11.3 us
    all_gather x1, local copies, waits for them, and re-layouts, fast(): t = lax.all_gather(x.transpose(1, 0, 2, 3), 'row', axis=0)  6.5 us
  transfers between devices with their start and end apart: 2, of which 1 were waited for; matrix products, arithmetic and copies ran while one was open for 1% of the time, Pallas kernels for 26%

profile of v2, /device:TPU:1, one launch (start us, length us, event | category | flops | bytes accessed | tf_op | source)
XLA Modules:
  0.0 274.9 jit_solution(4093745566630601489)
XLA Ops:
  6.5 1.5 copy.23
  8.3 0.2 reshape.309
  8.7 15.2 %all_to_all.5 = f32[4,5,8,1280]{3,2,1,0:T(8,128)} all-to-all(f32[4,5,8,1280]{3,2,1,0:T(8,128)S(1)} %maximum_bitcast_fusion), channel_id=1, replica_groups=mesh['row'=8,'col'=4] {'col'}, dimensions={0} | all-to-all | bytes 1638400 | tf_op jit(solution)/shard_map/all_to_all | solution.py:509
  24.0 1.8 multiply_subtract_fusion
  25.9 0.9 reshape.300
  27.2 64.9 %all-gather.5.cloned.1.call-done = f32[40,4,8,1280]{3,2,0,1:T(8,128)} async-done(((f32[5,4,8,1280]{3,2,0,1:T(8,128)}), f32[40,4,8,1280]{3,2,0,1:T(8,128)}) %all-gather.5.cloned.1.call-update) | async-done | bytes 6553616 | tf_op jit(solution)/shard_map/all_gather | solution.py:510
  92.0 6.5 %copy.26 = f32[40,4,8,1280]{3,2,1,0:T(8,128)} copy(f32[40,4,8,1280]{3,2,0,1:T(8,128)} %all-gather.5.cloned.1.call-done) | data formatting | bytes 13107200 | tf_op jit(solution)/shard_map/all_gather | solution.py:510
  98.5 8.3 %shard_map.83 = f32[32,256]{1,0:T(8,128)} custom-call(f32[2,16,40,160]{3,2,1,0:T(8,128)} %v_ref.3, f32[8,5,4,8,1280]{4,3,2,1,0:T(8,128)} %bitcast.47), custom_call_target="tpu_custom_call" | custom-call | flops 314572800 | bytes 819200 | tf_op jit(solution)/shard_map/pallas_call | solution.py:204
  106.8 70.6 %shard_map.82.part_ref = f32[3200,256]{1,0:T(8,128)} custom-call(f32[20,160,40,160]{3,2,1,0:T(8,128)} %v_ref.2, f32[8,5,4,8,1280]{4,3,2,1,0:T(8,128)} %bitcast.48), custom_call_target="tpu_custom_call" | custom-call | flops 31457280000 | bytes 81920000 | tf_op jit(solution)/shard_map/pallas_call | solution.py:204
  177.4 1.3 reduce_sum.9
  178.8 0.4 convolution_add_fusion.1
  179.1 1.0 fusion.2.mixing_ref
  180.1 11.3 %shard_map.84.part_ref = f32[4,8,2,4,3200]{4,3,2,1,0:T(4,128)} custom-call(f32[3200,256]{1,0:T(8,128)} %shard_map.82.part_ref, f32[8,5,4,8,1280]{4,3,2,1,0:T(8,128)} %bitcast.49, f32[256,256]{1,0:T(8,128)} %fusion.2.mixing_ref), custom_call_target="tpu_custom_call" | custom-call | tf_op jit(solution)/shard_map/pallas_call | solution.py:295
  191.4 1.9 copy-done.1
  193.3 62.3 %shard_map.85 = (f32[8,2,4,3200]{3,2,1,0:T(4,128)S(1)}, f32[8,2,4,3200]{3,2,1,0:T(4,128)S(1)}) custom-call(f32[4,8,2,4,3200]{4,3,2,1,0:T(4,128)S(1)} %copy-done.1), custom_call_target="tpu_custom_call" | custom-call | tf_op jit(solution)/shard_map/pallas_call | solution.py:460
  255.8 0.8 reshape.303
  256.6 2.1 copy.30
  258.6 2.5 copy.32
  261.2 1.0 copy.27
  262.2 1.9 reshape.301
  264.2 1.0 copy.28
  265.2 0.3 copy-done.2
  265.5 0.7 convolution_add_fusion
  266.2 1.9 fusion.1
  (29 shorter events, 1.0 us)
Async XLA Ops:
  6.5 258.6 %copy-start = (f32[160,160]{1,0:T(8,128)S(1)}, f32[160,160]{1,0:T(8,128)}, u32[]{:S(2)}) copy-start(f32[160,160]{1,0:T(8,128)} %param.13) | copy-start | bytes 307204
  6.5 85.5 %all-gather.5.cloned.1.call-start = ((), (), s32[]{:S(2)}) async-start(), calls=%async_computation.1 | async-start | bytes 7372800 | tf_op jit(solution)/shard_map/all_gather | solution.py:510
  8.7 15.3 %copy-start.3 = (f32[16,16]{1,0:T(8,128)S(1)}, f32[16,16]{1,0:T(8,128)}, u32[]{:S(2)}) copy-start(f32[16,16]{1,0:T(8,128)} %param.12) | copy-start | bytes 3076
  23.9 153.5 %all-gather.7.cloned.1.call-start = ((), (), s32[]{:S(2)}) async-start(), calls=%async_computation.2 | async-start | bytes 1081344 | tf_op jit(solution)/shard_map/all_gather | solution.py:513
  25.9 1.0 copy-start.5
  25.9 1.2 copy-start.4
  191.4 1.9 copy-start.1
  264.1 1.3 copy-start.2
Sparse Core Ops, SparseCore 0:
  24.1 67.9 all-gather.4
  106.9 52.3 all-gather.6

commit v3 on v2

--- a/solution.py
+++ b/solution.py
@@ -116,19 +116,45 @@
     return lax.dot_general(a, b, (dims, ((), ())), preferred_element_type=F32)
 
 
-def contract_kernel(take, slots, v_ref, t_ref, o_ref, buf, rest, spread, high, low, acc, w_high, w_low, sem):
+MESH = pl.DeviceIdType.MESH
+
+
+def remote(source, target, send, recv, r, q):
+    return pltpu.make_async_remote_copy(
+        src_ref=source, dst_ref=target, send_sem=send, recv_sem=recv, device_id=(r, q), device_id_type=MESH
+    )
+
+
+def greet(row, col, rows_n, cols_n):
+    barrier = pltpu.get_barrier_semaphore()
+    for k in range(1, cols_n):
+        pl.semaphore_signal(barrier, inc=1, device_id=(row, (col + k) % cols_n), device_id_type=MESH)
+    for k in range(1, rows_n):
+        pl.semaphore_signal(barrier, inc=1, device_id=((row + k) % rows_n, col), device_id_type=MESH)
+    pl.semaphore_wait(barrier, cols_n - 1 + rows_n - 1)
+
+
+def ladder_kernel(
+    take, slots, x_ref, v_ref, e_ref, t_ref, o_ref, chi_ref,
+    buf, rest, e_main, e_rest, e_spread, e_high, e_low, chi_sum, chi_got, spread, high, low, w_high, w_low,
+    sem, own, send_a, recv_a, send_u, recv_u, send_d, recv_d, send_c, recv_c, send_p, recv_p, send_r, recv_r,
+):
     a_count, b_count, c_count, virtual = v_ref.shape
-    group = buf.shape[4 - 1]
-    lanes = buf.shape[4]
+    rows_n, chunks, cols_n, n, width = t_ref.shape
+    levels = rows_n // 2
+    row, col = lax.axis_index("row"), lax.axis_index("col")
+    level, core = row // 2, row % 2
+    twin = row + 1 - 2 * core
+    group, lanes = buf.shape[3], buf.shape[4]
     tail = virtual - lanes
     rows = take * b_count
-    chunks = c_count // group
     blocks = a_count // take
     steps = chunks * blocks
     per = lanes // tail
-    width = t_ref.shape[-1]
-
-    def copies(step):
+    few = e_ref.shape[0] * e_ref.shape[1]
+    dims = ((1,), (1,))
+
+    def fetch(step):
         slot = lax.rem(step, slots)
         chunk, block = step // blocks, lax.rem(step, blocks)
         source = v_ref.at[
@@ -139,41 +165,127 @@
             pltpu.make_async_copy(source.at[:, :, :, pl.ds(lanes, tail)], rest.at[slot], sem.at[slot, 1]),
         )
 
-    for step in range(min(slots - 1, steps)):
-        for copy in copies(step):
+    def fetch_few():
+        return (
+            pltpu.make_async_copy(e_ref.at[:, :, :, pl.ds(0, lanes)], e_main, own.at[chunks]),
+            pltpu.make_async_copy(e_ref.at[:, :, :, pl.ds(lanes, tail)], e_rest, own.at[chunks + 1]),
+        )
+
+    def keep(c):
+        return pltpu.make_async_copy(x_ref.at[col, c], t_ref.at[row, c, col], own.at[c])
+
+    def deal(k, c):
+        q = (col + k) % cols_n
+        return remote(x_ref.at[q, c], t_ref.at[row, c, col], send_a.at[c, k], recv_a.at[c, k], row, q)
+
+    def dealt(k, c):
+        q = (col + cols_n - k) % cols_n
+        return remote(x_ref.at[col, c], t_ref.at[row, c, q], send_a.at[c, k], recv_a.at[c, k], row, q)
+
+    def up(k, c):
+        at = t_ref.at[jnp.maximum(row - 2 * k, core), c]
+        return remote(at, at, send_u.at[c, k], recv_u.at[c, k], jnp.minimum(row + 2, rows_n - 2 + core), col)
+
+    def down(k, c):
+        at = t_ref.at[jnp.minimum(row + 2 * k, rows_n - 2 + core), c]
+        return remote(at, at, send_d.at[c, k], recv_d.at[c, k], jnp.maximum(row - 2, core), col)
+
+    def came_up(k, c):
+        at = t_ref.at[jnp.maximum(row - 2 * k, core), c]
+        return remote(at, at, send_u.at[c, k - 1], recv_u.at[c, k - 1], jnp.maximum(row - 2, core), col)
+
+    def came_down(k, c):
+        at = t_ref.at[jnp.minimum(row + 2 * k, rows_n - 2 + core), c]
+        return remote(at, at, send_d.at[c, k - 1], recv_d.at[c, k - 1], jnp.minimum(row + 2, rows_n - 2 + core), col)
+
+    def share(m, c):
+        at = t_ref.at[2 * m + core, c]
+        return remote(at, at, send_c.at[c, m], recv_c.at[c, m], twin, col)
+
+    def shared(m, c):
+        at = t_ref.at[2 * m + 1 - core, c]
+        return remote(at, at, send_c.at[c, m], recv_c.at[c, m], twin, col)
+
+    def open_up(c):
+        keep(c).wait()
+        for k in range(1, cols_n):
+            dealt(k, c).wait_recv()
+
+        @pl.when(level < levels - 1)
+        def _():
+            up(0, c).start()
+
+        @pl.when(level > 0)
+        def _():
+            down(0, c).start()
+
+        share(level, c).start()
+
+    def relay(k, c):
+        @pl.when(level >= k)
+        def _():
+            came_up(k, c).wait_recv()
+
+            @pl.when(level < levels - 1)
+            def _():
+                up(k, c).start()
+
+            share(level - k, c).start()
+
+        @pl.when(level + k <= levels - 1)
+        def _():
+            came_down(k, c).wait_recv()
+
+            @pl.when(level > 0)
+            def _():
+                down(k, c).start()
+
+            share(level + k, c).start()
+
+    def settle(c):
+        for m in range(levels):
+            shared(m, c).wait_recv()
+
+    def plane(k):
+        q = (col + k) % cols_n
+        return remote(chi_sum, chi_got.at[k], send_p.at[k], recv_p.at[k], row, q)
+
+    def column(k):
+        r = (row + k) % rows_n
+        return remote(chi_ref.at[row], chi_ref.at[row], send_r.at[k], recv_r.at[k], r, col)
+
+    def columned(k):
+        r = (row + rows_n - k) % rows_n
+        return remote(chi_ref.at[r], chi_ref.at[r], send_r.at[k], recv_r.at[k], r, col)
+
+    for step in range(slots - 1):
+        for copy in fetch(step):
             copy.start()
-    acc[...] = jnp.zeros_like(acc)
-    lane = lax.broadcasted_iota(jnp.int32, (rows, lanes), 1)
-
-    def body(step, _):
-        slot = lax.rem(step, slots)
-        chunk, block = step // blocks, lax.rem(step, blocks)
-        for copy in copies(step):
-            copy.wait()
-
-        @pl.when(step + slots - 1 < steps)
-        def _():
-            for copy in copies(step + slots - 1):
-                copy.start()
-
-        @pl.when(block == 0)
-        def _():
-            for r in range(t_ref.shape[0]):
-                for q in range(t_ref.shape[2]):
-                    n = t_ref.shape[3]
-                    at = (r * t_ref.shape[2] + q) * n
-                    hi, lo = split(t_ref[r, chunk, q])
-                    w_high[at : at + n, :] = hi
-                    w_low[at : at + n, :] = lo
-
-        main = buf.at[slot].reshape(rows * group, lanes)
-        spread[:, pl.ds(0, tail)] = rest.at[slot].reshape(rows * group, tail)[...]
+    for copy in fetch_few():
+        copy.start()
+    greet(row, col, rows_n, cols_n)
+    for c in range(chunks):
+        keep(c).start()
+        for k in range(1, cols_n):
+            deal(k, c).start()
+    o_ref[...] = jnp.zeros_like(o_ref)
+    chi_sum[...] = jnp.zeros_like(chi_sum)
+    for copy in fetch_few():
+        copy.wait()
+    open_up(0)
+    open_up(1)
+    for k in range(1, levels):
+        relay(k, 0)
+    settle(0)
+
+    def lay(main, spread, start, stride, count, high, low):
+        lane = lax.broadcasted_iota(jnp.int32, (count, lanes), 1)
         packed = None
         for c in range(group):
-            hi, lo = split(main[pl.ds(c, rows, stride=group), :])
+            hi, lo = split(main[pl.ds(start + c, count, stride=stride), :])
             high[:, c * lanes : (c + 1) * lanes] = hi
             low[:, c * lanes : (c + 1) * lanes] = lo
-            piece = spread[pl.ds(c, rows, stride=group), :]
+            piece = spread[pl.ds(start + c, count, stride=stride), :]
             k = c % per
             packed = piece if k == 0 else jnp.where(lane < tail * k, packed, pltpu.roll(piece, tail * k, 1))
             if k == per - 1:
@@ -181,47 +293,149 @@
                 hi, lo = split(packed)
                 high[:, at : at + lanes] = hi
                 low[:, at : at + lanes] = lo
-        dims = ((1,), (1,))
-        acc[block] += (
+
+    def triple(high, low):
+        return (
             product(high[...], w_high[...], dims)
             + product(low[...], w_high[...], dims)
             + product(high[...], w_low[...], dims)
         )
+
+    e_spread[:, pl.ds(0, tail)] = e_rest.reshape(few * c_count, tail)[...]
+
+    def body(step, _):
+        slot = lax.rem(step, slots)
+        chunk, block = step // blocks, lax.rem(step, blocks)
+        for copy in fetch(step):
+            copy.wait()
+
+        @pl.when(step + slots - 1 < steps)
+        def _():
+            for copy in fetch(step + slots - 1):
+                copy.start()
+
+        @pl.when(block == 0)
+        def _():
+            @pl.when(chunk + 1 < chunks)
+            def _():
+                relay(1, chunk + 1)
+
+            @pl.when(chunk + 2 < chunks)
+            def _():
+                open_up(chunk + 2)
+
+            for r in range(rows_n):
+                for q in range(cols_n):
+                    at = (r * cols_n + q) * n
+                    hi, lo = split(t_ref[r, chunk, q])
+                    w_high[at : at + n, :] = hi
+                    w_low[at : at + n, :] = lo
+            lay(
+                e_main.reshape(few * c_count, lanes), e_spread, chunk * group, c_count, few, e_high, e_low
+            )
+            chi_sum[...] += triple(e_high, e_low)
+
+            @pl.when(chunk == chunks - 1)
+            def _():
+                for k in range(1, cols_n):
+                    plane(k).start()
+
+        @pl.when(chunk + 1 < chunks)
+        def _():
+            for k in range(2, levels):
+                @pl.when(block == min(2 * (k - 1), blocks - 1))
+                def _():
+                    relay(k, chunk + 1)
+
+        @pl.when((chunk == chunks - 1) & (block == 2))
+        def _():
+            total = chi_sum[...]
+            for k in range(1, cols_n):
+                plane(k).wait_recv()
+                total = total + chi_got[k]
+            chi_ref[row] = total
+            for k in range(1, rows_n):
+                column(k).start()
+
+        spread[:, pl.ds(0, tail)] = rest.at[slot].reshape(rows * group, tail)[...]
+        lay(buf.at[slot].reshape(rows * group, lanes), spread, 0, group, rows, high, low)
+        o_ref[pl.ds(pl.multiple_of(block * rows, rows), rows), :] += triple(high, low)
+
+        @pl.when((block == blocks - 1) & (chunk + 1 < chunks))
+        def _():
+            settle(chunk + 1)
+
         return 0
 
     lax.fori_loop(0, steps, body, 0)
-    for block in range(blocks):
-        o_ref[block * rows : (block + 1) * rows, :] = acc[block]
-
-
-def contract(v, t, take, slots):
+    for k in range(1, cols_n):
+        plane(k).wait_send()
+    for k in range(1, rows_n):
+        column(k).wait_send()
+        columned(k).wait_recv()
+    for c in range(chunks):
+        for k in range(1, cols_n):
+            deal(k, c).wait_send()
+        for m in range(levels):
+            share(m, c).wait_send()
+        for k in range(levels - 1):
+            @pl.when((level >= k) & (level < levels - 1))
+            def _():
+                up(k, c).wait_send()
+
+            @pl.when((level + k <= levels - 1) & (level > 0))
+            def _():
+                down(k, c).wait_send()
+
+
+def ladder(x, v, e, rows_n, take, slots):
     a_count, b_count, c_count, virtual = v.shape
-    rows_n, chunks, cols_n, n, width = t.shape
+    cols_n, chunks, n, width = x.shape
     pairs = rows_n * cols_n * n
     group, lanes = c_count // chunks, 128
+    tail = virtual - lanes
     rows = take * b_count
-    shape = (a_count * b_count, pairs)
+    few = e.shape[0] * e.shape[1]
+    levels = rows_n // 2
+    dma = pltpu.SemaphoreType.DMA
+    vmem = pl.BlockSpec(memory_space=pltpu.VMEM)
+    hbm = pl.BlockSpec(memory_space=pl.ANY)
     return pl.pallas_call(
-        functools.partial(contract_kernel, take, slots),
-        out_shape=jax.ShapeDtypeStruct(shape, F32),
-        in_specs=[pl.BlockSpec(memory_space=pl.ANY), pl.BlockSpec(memory_space=pltpu.VMEM)],
-        out_specs=pl.BlockSpec(memory_space=pltpu.VMEM),
+        functools.partial(ladder_kernel, take, slots),
+        out_shape=[
+            jax.ShapeDtypeStruct((rows_n, chunks, cols_n, n, width), F32),
+            jax.ShapeDtypeStruct((a_count * b_count, pairs), F32),
+            jax.ShapeDtypeStruct((rows_n, few, pairs), F32),
+        ],
+        in_specs=[vmem, hbm, hbm],
+        out_specs=[vmem] * 3,
         scratch_shapes=[
             pltpu.VMEM((slots, take, b_count, group, lanes), F32),
-            pltpu.VMEM((slots, take, b_count, group, virtual - lanes), F32),
+            pltpu.VMEM((slots, take, b_count, group, tail), F32),
+            pltpu.VMEM(e.shape[:3] + (lanes,), F32),
+            pltpu.VMEM(e.shape[:3] + (tail,), F32),
+            pltpu.VMEM((few * c_count, lanes), F32),
+            pltpu.VMEM((few, width), BF16),
+            pltpu.VMEM((few, width), BF16),
+            pltpu.VMEM((few, pairs), F32),
+            pltpu.VMEM((cols_n, few, pairs), F32),
             pltpu.VMEM((rows * group, lanes), F32),
             pltpu.VMEM((rows, width), BF16),
             pltpu.VMEM((rows, width), BF16),
-            pltpu.VMEM((a_count // take, rows, pairs), F32),
             pltpu.VMEM((pairs, width), BF16),
             pltpu.VMEM((pairs, width), BF16),
-            pltpu.SemaphoreType.DMA((slots, 2)),
+            dma((slots, 2)), dma((chunks + 2,)),
+            dma((chunks, cols_n)), dma((chunks, cols_n)),
+            dma((chunks, levels)), dma((chunks, levels)),
+            dma((chunks, levels)), dma((chunks, levels)),
+            dma((chunks, levels)), dma((chunks, levels)),
+            dma((cols_n,)), dma((cols_n,)),
+            dma((rows_n,)), dma((rows_n,)),
         ],
-        compiler_params=pltpu.CompilerParams(vmem_limit_bytes=60 << 20),
-        cost_estimate=pl.CostEstimate(
-            flops=6 * v.size * pairs, bytes_accessed=4 * v.size, transcendentals=0
+        compiler_params=pltpu.CompilerParams(
+            collective_id=0, has_side_effects=True, vmem_limit_bytes=60 << 20
         ),
-    )(v, t)
+    )(x, v, e)
 
 
 def hole_kernel(a_count, c_count, virtual, part_ref, t_ref, mixing_ref, o_ref, w_high, w_low, picked, add):
@@ -506,12 +720,8 @@
         ],
         axis=-1,
     ).transpose(1, 2, 0, 3)
-    x = lax.all_to_all(x, "col", split_axis=0, concat_axis=0, tiled=True)
-    t = lax.all_gather(x.transpose(1, 0, 2, 3), "row", axis=0)
-
-    chi_part = contract(exchange_ints, t, exchange_ints.shape[0], 3)
-    chi_all = lax.all_gather(chi_part, ("row", "col"), axis=0)
-    chi = chi_all.reshape(rows_n, cols_n, -1, pairs).sum(axis=1).reshape(pairs, pairs)
+    t, part, chi = ladder(x, vvvv, exchange_ints, rows_n, 4, 3)
+    chi = chi.reshape(pairs, pairs)
     delta = jnp.eye(occupied, dtype=fock_occ.dtype)
     known = hole_ints - delta[:, None, :, None] * fock_occ[None, :, None, :]
     highest = lax.Precision.HIGHEST
@@ -526,7 +736,6 @@
     move = (spots[:, None] == place(two, one)[None, :]).astype(F32)
     known = jnp.dot(known.reshape(pairs, pairs), turn, precision=highest)
 
-    part = contract(vvvv, t, 4, 3)
 
     mixing = jnp.dot(move, chi + known, precision=highest)
     part = hole(part, t, mixing, a_count, c_count, virtual)

time: 275 us -> 197 us (0.72)
  the two profiles are of different devices: /device:TPU:1 before, /device:TPU:25 now
where the time goes in v3:
time: 197 us
  Pallas kernels  175 us (89%)
  local copies, waits for them, and re-layouts  14.7 us (7%)
  matrix products  3.97 us (2%)
  other arithmetic  2.96 us (2%)
    pallas_call x1, Pallas kernels, ladder(): pl.pallas_call(functools.partial(ladder_kernel, take, slots), out_shape=[...  99.4 us
    pallas_call x1, Pallas kernels, exchange(): pl.pallas_call(exchange_kernel, out_shape=[jax.ShapeDtypeStruct((rows_n,)...  64.3 us
    pallas_call x1, Pallas kernels, hole(): pl.pallas_call(functools.partial(hole_kernel, a_count, c_count, virtual),...  11.2 us

profile of v3, /device:TPU:25, one launch (start us, length us, event | category | flops | bytes accessed | tf_op | source)
XLA Modules:
  0.0 196.7 jit_solution(2666000869371140543)
XLA Ops:
  0.0 1.5 copy.23
  1.6 0.4 copy.42
  2.0 0.2 reshape.302
  2.2 0.1 copy.37
  2.3 0.9 maximum_bitcast_fusion.x_ref
  3.3 99.4 %shard_map.82 = (f32[8,5,4,8,1280]{4,3,2,1,0:T(8,128)}, f32[3200,256]{1,0:T(8,128)}, f32[8,32,256]{2,1,0:T(8,128)}) custom-call(f32[4,5,8,1280]{3,2,1,0:T(8,128)} %maximum_bitcast_fusion.x_ref, f32[20,160,40,160]{3,2,1,0:T(8,128)} %v_ref.1, f32[2,16,40,160]{3,2,1,0:T(8,128)} %e_ref.1), custom_call_target="tpu_custom_call" | custom-call | tf_op jit(solution)/shard_map/pallas_call | solution.py:403
  102.7 1.8 multiply_subtract_fusion
  104.6 0.9 reshape.296
  105.5 0.4 convolution_add_fusion.1
  105.9 1.0 fusion.2.mixing_ref
  106.9 11.2 %shard_map.83.part_ref = f32[4,8,2,4,3200]{4,3,2,1,0:T(4,128)} custom-call(f32[3200,256]{1,0:T(8,128)} %get-tuple-element.10.part_ref, f32[8,5,4,8,1280]{4,3,2,1,0:T(8,128)} %get-tuple-element.11.t_ref, f32[256,256]{1,0:T(8,128)} %fusion.2.mixing_ref), custom_call_target="tpu_custom_call" | custom-call | tf_op jit(solution)/shard_map/pallas_call | solution.py:509
  118.1 1.9 copy-done.1
  120.1 64.3 %shard_map.84 = (f32[8,2,4,3200]{3,2,1,0:T(4,128)S(1)}, f32[8,2,4,3200]{3,2,1,0:T(4,128)S(1)}) custom-call(f32[4,8,2,4,3200]{4,3,2,1,0:T(4,128)S(1)} %copy-done.1), custom_call_target="tpu_custom_call" | custom-call | tf_op jit(solution)/shard_map/pallas_call | solution.py:674
  184.4 0.2 copy.28
  184.5 0.8 reshape.299
  185.3 2.1 %copy.29 = f32[2,2,2,160,8,20]{3,0,5,4,2,1:T(2,128)} copy(f32[2,2,2,160,8,20]{3,5,4,0,2,1:T(8,128)S(1)} %bitcast.43) | data formatting | bytes 1638400 | tf_op jit(solution)/shard_map/transpose | solution.py:746
  187.4 3.8 %copy.31 = f32[2,4,160,160]{3,2,1,0:T(8,128)} copy(f32[2,4,160,160]{2,0,3,1:T(2,128)} %bitcast.47) | data formatting | bytes 1638400 | tf_op jit(solution)/shard_map/reshape | solution.py:746
  191.1 0.2 copy.26
  191.3 0.8 reshape.297
  192.1 1.0 copy.27
  193.1 0.3 copy-done.2
  193.4 0.4 copy-done.3
  193.8 0.7 convolution_add_fusion
  194.8 1.9 fusion.1
  (22 shorter events, 0.5 us)
Async XLA Ops:
  0.0 193.1 %copy-start = (f32[160,160]{1,0:T(8,128)S(1)}, f32[160,160]{1,0:T(8,128)}, u32[]{:S(2)}) copy-start(f32[160,160]{1,0:T(8,128)} %param.13) | copy-start | bytes 307204
  3.3 99.4 %copy-start.5 = (f32[16,16]{1,0:T(8,128)S(1)}, f32[16,16]{1,0:T(8,128)}, u32[]{:S(2)}) copy-start(f32[16,16]{1,0:T(8,128)} %param.12) | copy-start | bytes 3076
  104.5 1.0 copy-start.4
  118.1 1.9 copy-start.1
  192.1 1.3 copy-start.2
  192.1 1.7 copy-start.3
  193.8 0.7 copy-start.7
  193.8 1.0 copy-start.6

commit v4 on v1

v4 whole, which is shorter than its diff:
```python
import functools

import jax
import jax.numpy as jnp
from jax import lax
from jax.experimental import pallas as pl
from jax.experimental.pallas import tpu as pltpu
from jax.sharding import PartitionSpec as P

def finish(raw, amplitudes, fock_vir, eps_occ, eps_vir):
    high = lax.Precision.HIGH
    rows_n = lax.axis_size("row")
    cols_n = lax.axis_size("col")
    row = lax.axis_index("row")
    col = lax.axis_index("col")
    first_count, second_count, virtual = amplitudes.shape[:3]
    ratio = second_count // first_count
    others = []
    for turn in range(ratio):
        route = []
        for r in range(rows_n):
            for q in range(cols_n):
                m = (r + turn) % ratio
                route.append((r * cols_n + q, (q * ratio + m) * cols_n + r // ratio))
        m = lax.rem(row + turn, ratio)
        block = lax.dynamic_slice_in_dim(raw, m * first_count, first_count, axis=1)
        others.append(lax.ppermute(block, ("row", "col"), route))
    stacked = jnp.stack(others)
    order = jnp.stack([lax.rem(row - m + ratio, ratio) for m in range(ratio)])
    other = stacked[order].reshape(ratio, first_count, first_count, virtual, virtual)
    other = other.transpose(2, 0, 1, 4, 3)
    other = other.reshape(first_count, second_count, virtual, virtual)
    total = raw.reshape(first_count, second_count, virtual, virtual) + other
    return close(total, amplitudes, fock_vir, eps_occ, eps_vir)


def close(total, amplitudes, fock_vir, eps_occ, eps_vir):
    high = lax.Precision.HIGH
    row = lax.axis_index("row")
    col = lax.axis_index("col")
    first_count, second_count = amplitudes.shape[:2]
    total = total + jnp.einsum("ijac,cb->ijab", amplitudes, fock_vir, precision=high)
    total = total + jnp.einsum("ac,ijcb->ijab", fock_vir, amplitudes, precision=high)
    energy_rows = lax.dynamic_slice_in_dim(eps_occ, row * first_count, first_count)
    energy_cols = lax.dynamic_slice_in_dim(eps_occ, col * second_count, second_count)
    denominator = (
        energy_rows[:, None, None, None]
        + energy_cols[None, :, None, None]
        - eps_vir[None, None, :, None]
        - eps_vir[None, None, None, :]
    )
    return total / denominator


def plain(amplitudes, vvvv, hole_ints, exchange_ints, fock_occ, fock_vir, eps_occ, eps_vir):
    high = lax.Precision.HIGH
    rows_n = lax.axis_size("row")
    cols_n = lax.axis_size("col")
    row = lax.axis_index("row")
    col = lax.axis_index("col")
    first_count, second_count, virtual = amplitudes.shape[:3]
    occupied = fock_occ.shape[0]
    pairs_n = occupied * occupied
    a_count = vvvv.shape[0]
    c_count = vvvv.shape[2]
    k_count = exchange_ints.shape[0]

    split = lax.all_to_all(amplitudes, "col", split_axis=2, concat_axis=1, tiled=True)
    split = split.reshape(first_count * occupied, c_count * virtual)
    gathered = lax.all_gather(split, "row", axis=0, tiled=True)
    gathered = gathered.reshape(occupied, occupied, c_count, virtual)

    chi_part = lax.dot_general(
        gathered, exchange_ints, (((2, 3), (2, 3)), ((), ())), precision=high
    )
    chi_part = chi_part.reshape(pairs_n, k_count * occupied).T
    chi_all = lax.all_gather(chi_part, ("row", "col"), axis=0)
    chi = chi_all.reshape(rows_n, cols_n, k_count * occupied, pairs_n).sum(axis=1)
    delta = jnp.eye(occupied, dtype=fock_occ.dtype)
    known = hole_ints - delta[:, None, :, None] * fock_occ[None, :, None, :]
    mixing = chi.reshape(pairs_n, pairs_n) + known.reshape(pairs_n, pairs_n)

    mine = lax.dynamic_slice_in_dim(gathered, row * a_count, a_count, axis=3)
    mine = mine.transpose(1, 0, 3, 2).reshape(pairs_n, a_count * c_count)
    placed = lax.all_gather(mine, "col", axis=0)
    placed = placed.reshape(cols_n, pairs_n, a_count, c_count).transpose(1, 2, 0, 3)
    placed = placed.reshape(pairs_n, a_count * virtual)

    part = lax.dot_general(gathered, vvvv, (((2, 3), (2, 3)), ((), ())), precision=high)
    part = part.transpose(1, 0, 2, 3).reshape(occupied, occupied, a_count * virtual)
    raw = lax.psum_scatter(part, "col", scatter_dimension=0, tiled=True)
    chosen = lax.dynamic_slice_in_dim(
        mixing.reshape(pairs_n, occupied, occupied), col * second_count, second_count, axis=2
    )
    chosen = chosen.transpose(0, 2, 1).reshape(pairs_n, second_count * occupied)
    hole = lax.dot_general(chosen, placed, (((0,), (0,)), ((), ())), precision=high)
    raw = raw + hole.reshape(raw.shape)
    raw = raw.reshape(second_count, rows_n, first_count, a_count * virtual)
    raw = raw.transpose(1, 2, 0, 3)
    raw = lax.all_to_all(raw, "row", split_axis=0, concat_axis=0, tiled=True)
    raw = raw.transpose(1, 2, 0, 3).reshape(first_count, second_count, virtual * virtual)

    return finish(raw, amplitudes, fock_vir, eps_occ, eps_vir)


F32 = jnp.float32
BF16 = jnp.bfloat16


def split(x):
    high = x.astype(BF16)
    return high, (x - high.astype(F32)).astype(BF16)


def product(a, b, dims):
    return lax.dot_general(a, b, (dims, ((), ())), preferred_element_type=F32)


MESH = pl.DeviceIdType.MESH


def remote(source, target, send, recv, r, q):
    return pltpu.make_async_remote_copy(
        src_ref=source, dst_ref=target, send_sem=send, recv_sem=recv, device_id=(r, q), device_id_type=MESH
    )


def greet(row, col, rows_n, cols_n):
    barrier = pltpu.get_barrier_semaphore()
    for k in range(1, cols_n):
        pl.semaphore_signal(barrier, inc=1, device_id=(row, (col + k) % cols_n), device_id_type=MESH)
    for k in range(1, rows_n):
        pl.semaphore_signal(barrier, inc=1, device_id=((row + k) % rows_n, col), device_id_type=MESH)
    pl.semaphore_wait(barrier, cols_n - 1 + rows_n - 1)


def whole_kernel(
    take, slots, late, x_ref, v_ref, e_ref, known_ref, move_ref, straight_ref, turned_ref,
    t_ref, o_ref, chi_ref, buf, rest, e_main, e_rest, e_spread, e_high, e_low, chi_sum, chi_got,
    spread, high, low, w_high, w_low, picked, part_ref, got, last, onward, sums, middle,
    sem, own, send_a, recv_a, send_u, recv_u, send_d, recv_d, send_c, recv_c, send_p, recv_p, send_r, recv_r,
    xsend_a, xrecv_a, xsend_b, xrecv_b, xsend_c, xrecv_c, xsend_d, xrecv_d, xsend_e, xrecv_e, xown,
):
    a_count, b_count, c_count, virtual = v_ref.shape
    rows_n, chunks, cols_n, n, width = t_ref.shape
    levels = rows_n // 2
    row, col = lax.axis_index("row"), lax.axis_index("col")
    level, core = row // 2, row % 2
    twin = row + 1 - 2 * core
    group, lanes = buf.shape[3], buf.shape[4]
    tail = virtual - lanes
    rows = take * b_count
    blocks = a_count // take
    steps = chunks * blocks
    per = lanes // tail
    few = e_ref.shape[0] * e_ref.shape[1]
    pairs = rows_n * cols_n * n
    early = chunks - late
    dims = ((1,), (1,))
    flips = (col + 1 - 2 * (col % 2), (col + 2) % 4)
    far = 3 - col

    def where(step):
        after = step - early * blocks
        is_late = step >= early * blocks
        chunk = jnp.where(is_late, early + lax.rem(jnp.maximum(after, 0), late), step // blocks)
        block = jnp.where(is_late, jnp.maximum(after, 0) // late, lax.rem(step, blocks))
        return chunk, block

    def fetch(step):
        slot = lax.rem(step, slots)
        chunk, block = where(step)
        source = v_ref.at[
            pl.ds(block * take, take), :, pl.ds(pl.multiple_of(chunk * group, group), group), :
        ]
        return (
            pltpu.make_async_copy(source.at[:, :, :, pl.ds(0, lanes)], buf.at[slot], sem.at[slot, 0]),
            pltpu.make_async_copy(source.at[:, :, :, pl.ds(lanes, tail)], rest.at[slot], sem.at[slot, 1]),
        )

    def fetch_few():
        return (
            pltpu.make_async_copy(e_ref.at[:, :, :, pl.ds(0, lanes)], e_main, own.at[chunks]),
            pltpu.make_async_copy(e_ref.at[:, :, :, pl.ds(lanes, tail)], e_rest, own.at[chunks + 1]),
        )

    def keep(c):
        return pltpu.make_async_copy(x_ref.at[col, c], t_ref.at[row, c, col], own.at[c])

    def deal(k, c):
        q = (col + k) % cols_n
        return remote(x_ref.at[q, c], t_ref.at[row, c, col], send_a.at[c, k], recv_a.at[c, k], row, q)

    def dealt(k, c):
        q = (col + cols_n - k) % cols_n
        return remote(x_ref.at[col, c], t_ref.at[row, c, q], send_a.at[c, k], recv_a.at[c, k], row, q)

    def up(k, c):
        at = t_ref.at[jnp.maximum(row - 2 * k, core), c]
        return remote(at, at, send_u.at[c, k], recv_u.at[c, k], jnp.minimum(row + 2, rows_n - 2 + core), col)

    def down(k, c):
        at = t_ref.at[jnp.minimum(row + 2 * k, rows_n - 2 + core), c]
        return remote(at, at, send_d.at[c, k], recv_d.at[c, k], jnp.maximum(row - 2, core), col)

    def came_up(k, c):
        at = t_ref.at[jnp.maximum(row - 2 * k, core), c]
        return remote(at, at, send_u.at[c, k - 1], recv_u.at[c, k - 1], jnp.maximum(row - 2, core), col)

    def came_down(k, c):
        at = t_ref.at[jnp.minimum(row + 2 * k, rows_n - 2 + core), c]
        return remote(at, at, send_d.at[c, k - 1], recv_d.at[c, k - 1], jnp.minimum(row + 2, rows_n - 2 + core), col)

    def share(m, c):
        at = t_ref.at[2 * m + core, c]
        return remote(at, at, send_c.at[c, m], recv_c.at[c, m], twin, col)

    def shared(m, c):
        at = t_ref.at[2 * m + 1 - core, c]
        return remote(at, at, send_c.at[c, m], recv_c.at[c, m], twin, col)

    def open_up(c):
        keep(c).wait()
        for k in range(1, cols_n):
            dealt(k, c).wait_recv()

        @pl.when(level < levels - 1)
        def _():
            up(0, c).start()

        @pl.when(level > 0)
        def _():
            down(0, c).start()

        share(level, c).start()

    def relay(k, c):
        @pl.when(level >= k)
        def _():
            came_up(k, c).wait_recv()

            @pl.when(level < levels - 1)
            def _():
                up(k, c).start()

            share(level - k, c).start()

        @pl.when(level + k <= levels - 1)
        def _():
            came_down(k, c).wait_recv()

            @pl.when(level > 0)
            def _():
                down(k, c).start()

            share(level + k, c).start()

    def settle(c):
        for m in range(levels):
            shared(m, c).wait_recv()

    def plane(k):
        q = (col + k) % cols_n
        return remote(chi_sum, chi_got.at[k], send_p.at[k], recv_p.at[k], row, q)

    def column(k):
        r = (row + k) % rows_n
        return remote(chi_ref.at[row], chi_ref.at[row], send_r.at[k], recv_r.at[k], r, col)

    def columned(k):
        r = (row + rows_n - k) % rows_n
        return remote(chi_ref.at[r], chi_ref.at[r], send_r.at[k], recv_r.at[k], r, col)

    for step in range(slots - 1):
        for copy in fetch(step):
            copy.start()
    for copy in fetch_few():
        copy.start()
    greet(row, col, rows_n, cols_n)
    for c in range(chunks):
        keep(c).start()
        for k in range(1, cols_n):
            deal(k, c).start()
    o_ref[...] = jnp.zeros_like(o_ref)
    chi_sum[...] = jnp.zeros_like(chi_sum)
    for copy in fetch_few():
        copy.wait()
    open_up(0)
    open_up(1)
    for k in range(1, levels):
        relay(k, 0)
    settle(0)

    def lay(main, spread, start, stride, count, high, low):
        lane = lax.broadcasted_iota(jnp.int32, (count, lanes), 1)
        packed = None
        for c in range(group):
            hi, lo = split(main[pl.ds(start + c, count, stride=stride), :])
            high[:, c * lanes : (c + 1) * lanes] = hi
            low[:, c * lanes : (c + 1) * lanes] = lo
            piece = spread[pl.ds(start + c, count, stride=stride), :]
            k = c % per
            packed = piece if k == 0 else jnp.where(lane < tail * k, packed, pltpu.roll(piece, tail * k, 1))
            if k == per - 1:
                at = (group + c // per) * lanes
                hi, lo = split(packed)
                high[:, at : at + lanes] = hi
                low[:, at : at + lanes] = lo

    def pair(k):
        return flips if k < rows_n // 2 else (flips[1], flips[0])

    def scatter(p, k):
        near = pair(k)[0]
        return [
            remote(part_ref.at[p, q, k], got.at[p, k, m], xsend_a.at[p, k, m], xrecv_a.at[p, k, m], row, near)
            for m, q in enumerate((near, far))
        ]

    def pass_on(p, k):
        return remote(onward.at[p, k], last.at[p, k], xsend_b.at[p, k], xrecv_b.at[p, k], row, pair(k)[1])

    def deliver(p, k):
        return remote(sums.at[p, k], straight_ref.at[row, p], xsend_c.at[p, k], xrecv_c.at[p, row], k, col)

    def delivered(p, k):
        return remote(sums.at[p, k], straight_ref.at[k, p], xsend_c.at[p, k], xrecv_c.at[p, k], k, col)

    def deliver_own(p, k):
        return pltpu.make_async_copy(sums.at[p, k], straight_ref.at[row, p], xown.at[p, 0])

    def cross(p, k):
        return remote(
            sums.at[p, k], middle.at[p, k % 2, col], xsend_d.at[p, k], xrecv_d.at[p, k % 2, col], row, k // 2
        )

    def crossed(p, m, q):
        return remote(sums.at[p, m], middle.at[p, m, q], xsend_d.at[p, m], xrecv_d.at[p, m, q], row, q)

    def cross_own(p, k):
        return pltpu.make_async_copy(sums.at[p, k], middle.at[p, k % 2, col], xown.at[p, 1 + k % 2])

    def fan(p, m, q, h):
        return remote(
            middle.at[p, m, q, h], turned_ref.at[row, p, m],
            xsend_e.at[p, m, q, h], xrecv_e.at[p, row, m], 2 * q + h, col,
        )

    def fanned(p, m, k):
        return remote(
            middle.at[p, m, k // 2, k % 2], turned_ref.at[k, p, m],
            xsend_e.at[p, m, k // 2, k % 2], xrecv_e.at[p, k, m], k, col,
        )

    def fan_own(p, m, q, h):
        return pltpu.make_async_copy(middle.at[p, m, q, h], turned_ref.at[row, p, m], xown.at[p, 3 + m])

    order = [k for m in range(rows_n // 2) for k in (m, rows_n // 2 + m)]

    def launch(p):
        turned = o_ref[pl.ds(pl.multiple_of(p * rows, rows), rows), :].T
        for r in range(rows_n):
            for q in range(cols_n):
                for h in range(2):
                    at = (r * cols_n + q) * n + h * n // 2
                    part_ref[p, q, r, h] = turned[at : at + n // 2, :]
        for k in order:
            for copy in scatter(p, k):
                copy.start()

    def first(p):
        for k in order:
            for copy in scatter(p, k):
                copy.wait_recv()
            onward[p, k] = part_ref[p, pair(k)[1], k] + got[p, k, 1]
            sums[p, k] = part_ref[p, col, k] + got[p, k, 0]
            pass_on(p, k).start()

    def second(p):
        for k in order:
            pass_on(p, k).wait_recv()
            sums[p, k] = sums[p, k] + last[p, k]

            @pl.when(col != k // 2)
            def _():
                cross(p, k).start()

            @pl.when(col == k // 2)
            def _():
                cross_own(p, k).start()

            @pl.when(row != k)
            def _():
                deliver(p, k).start()

            @pl.when(row == k)
            def _():
                deliver_own(p, k).start()

    def third(p):
        for k in order:
            m = k % 2

            @pl.when(col == k // 2)
            def _():
                cross_own(p, k).wait()
                for q in range(cols_n):
                    @pl.when(col != q)
                    def _():
                        crossed(p, m, q).wait_recv()

                    for h in range(2):
                        @pl.when(row != 2 * q + h)
                        def _():
                            fan(p, m, q, h).start()

                        @pl.when(row == 2 * q + h)
                        def _():
                            fan_own(p, m, q, h).start()

    def drain(p):
        for k in order:
            for copy in scatter(p, k):
                copy.wait_send()
            pass_on(p, k).wait_send()

            @pl.when(row != k)
            def _():
                deliver(p, k).wait_send()
                delivered(p, k).wait_recv()
                for m in range(2):
                    fan(p, m, k // 2, k % 2).wait_send()
                    fanned(p, m, k).wait_recv()

            @pl.when(row == k)
            def _():
                deliver_own(p, k).wait()
                for m in range(2):
                    fan_own(p, m, k // 2, k % 2).wait()

            @pl.when(col != k // 2)
            def _():
                cross(p, k).wait_send()

    def triple(high, low, w):
        return (
            product(high[...], w_high[w], dims)
            + product(low[...], w_high[w], dims)
            + product(high[...], w_low[w], dims)
        )

    e_spread[:, pl.ds(0, tail)] = e_rest.reshape(few * c_count, tail)[...]
    tall = -(-a_count // 16) * 16
    spot = row * a_count + lax.broadcasted_iota(jnp.int32, (tall, lanes), 0)
    lane = lax.broadcasted_iota(jnp.int32, (tall, lanes), 1)
    choose = jnp.where(spot == lane, 1.0, 0.0).astype(BF16)
    later = []
    for k in range(per):
        hit = (spot - lanes == lane - k * tail) & (lane >= k * tail) & (lane < (k + 1) * tail)
        later.append(jnp.where(hit, 1.0, 0.0).astype(BF16))

    def prepare(chunk, w):
        for r in range(rows_n):
            for q in range(cols_n):
                at = (r * cols_n + q) * n
                hi, lo = split(t_ref[r, chunk, q])
                w_high[w, at : at + n, :] = hi
                w_low[w, at : at + n, :] = lo
        for c in range(group):
            at = (group + c // per) * lanes
            total = None
            for ref in (w_high, w_low):
                value = product(choose, ref[w, :, c * lanes : (c + 1) * lanes], dims)
                value += product(later[c % per], ref[w, :, at : at + lanes], dims)
                total = value if total is None else total + value
            for half in range(pairs // lanes):
                picked[half, pl.ds(chunk * group + c, a_count, stride=c_count), :] = total[
                    :a_count, half * lanes : (half + 1) * lanes
                ]
        lay(e_main.reshape(few * c_count, lanes), e_spread, chunk * group, c_count, few, e_high, e_low)
        chi_sum[...] += triple(e_high, e_low, w)

    def multiply(step, block, w):
        slot = lax.rem(step, slots)
        for copy in fetch(step):
            copy.wait()

        @pl.when(step + slots - 1 < steps)
        def _():
            for copy in fetch(step + slots - 1):
                copy.start()

        spread[:, pl.ds(0, tail)] = rest.at[slot].reshape(rows * group, tail)[...]
        lay(buf.at[slot].reshape(rows * group, lanes), spread, 0, group, rows, high, low)
        o_ref[pl.ds(pl.multiple_of(block * rows, rows), rows), :] += triple(high, low, w)

    def opening(step, _):
        chunk, block = step // blocks, lax.rem(step, blocks)
        ahead = 1 + step // (levels - 1)

        @pl.when(ahead < chunks)
        def _():
            for k in range(1, levels):
                @pl.when(lax.rem(step, levels - 1) == k - 1)
                def _():
                    relay(k, ahead)

            @pl.when((lax.rem(step, levels - 1) == 0) & (ahead + 1 < chunks))
            def _():
                open_up(ahead + 1)

        @pl.when(block == 0)
        def _():
            prepare(chunk, 0)

        multiply(step, block, 0)

        @pl.when((block == blocks - 1) & (chunk + 1 < early))
        def _():
            settle(chunk + 1)

        return 0

    lax.fori_loop(0, early * blocks, opening, 0)
    for w in range(late):
        settle(early + w)
        prepare(early + w, w)
    for k in range(1, cols_n):
        plane(k).start()

    def hole():
        for k in range(1, rows_n):
            columned(k).wait_recv()
        turn_high = turn_low = None
        for r in range(rows_n):
            at = slice(r * few, (r + 1) * few)
            hi, lo = split(chi_ref[r] + known_ref[at, :])
            turn = move_ref[:, at]
            hi = product(turn, hi, ((1,), (0,)))
            lo = product(turn, lo, ((1,), (0,)))
            turn_high = hi if turn_high is None else turn_high + hi
            turn_low = lo if turn_low is None else turn_low + lo
        mix_high, mix_low = turn_high.astype(BF16), turn_low.astype(BF16)
        total = None
        for half in range(pairs // lanes):
            hi, lo = split(picked[half])
            at = slice(half * lanes, (half + 1) * lanes)
            value = (
                product(hi, mix_high[at, :], ((1,), (0,)))
                + product(lo, mix_high[at, :], ((1,), (0,)))
                + product(hi, mix_low[at, :], ((1,), (0,)))
            )
            total = value if total is None else total + value
        for a in range(a_count):
            at = pl.ds(pl.multiple_of(a * b_count + col * c_count, 8), c_count)
            o_ref[at, :] += total[a * c_count : (a + 1) * c_count, :]

    def closing(block, _):
        def inner(w, _):
            multiply(early * blocks + block * late + w, block, w)

            @pl.when((block == 0) & (w == 0))
            def _():
                total = chi_sum[...]
                for k in range(1, cols_n):
                    plane(k).wait_recv()
                    total = total + chi_got[k]
                chi_ref[row] = total
                for k in range(1, rows_n):
                    column(k).start()

            @pl.when((w == 0) & (block >= 1))
            def _():
                first(block - 1)

            return 0

        lax.fori_loop(0, late, inner, 0)

        @pl.when(block == 0)
        def _():
            hole()

        launch(block)

        @pl.when(block >= 1)
        def _():
            second(block - 1)

        @pl.when(block >= 2)
        def _():
            third(block - 2)

        return 0

    lax.fori_loop(0, blocks, closing, 0)
    third(blocks - 2)
    first(blocks - 1)
    second(blocks - 1)
    third(blocks - 1)
    lax.fori_loop(0, blocks, lambda p, _: (drain(p), 0)[1], 0)
    for k in range(1, cols_n):
        plane(k).wait_send()
    for k in range(1, rows_n):
        column(k).wait_send()
    for c in range(chunks):
        for k in range(1, cols_n):
            deal(k, c).wait_send()
        for m in range(levels):
            share(m, c).wait_send()
        for k in range(levels - 1):
            @pl.when((level >= k) & (level < levels - 1))
            def _():
                up(k, c).wait_send()

            @pl.when((level + k <= levels - 1) & (level > 0))
            def _():
                down(k, c).wait_send()


def whole(x, v, e, known, move, rows_n, take, slots, late):
    a_count, b_count, c_count, virtual = v.shape
    cols_n, chunks, n, width = x.shape
    pairs = rows_n * cols_n * n
    group, lanes = c_count // chunks, 128
    tail = virtual - lanes
    rows = take * b_count
    blocks = a_count // take
    few = e.shape[0] * e.shape[1]
    levels = rows_n // 2
    block = (2, n // 2, rows)
    dma = pltpu.SemaphoreType.DMA
    vmem = pl.BlockSpec(memory_space=pltpu.VMEM)
    hbm = pl.BlockSpec(memory_space=pl.ANY)
    return pl.pallas_call(
        functools.partial(whole_kernel, take, slots, late),
        out_shape=[jax.ShapeDtypeStruct((rows_n, blocks) + block, F32)] * 2,
        in_specs=[vmem, hbm, hbm, vmem, vmem],
        out_specs=[vmem] * 2,
        scratch_shapes=[
            pltpu.VMEM((rows_n, chunks, cols_n, n, width), F32),
            pltpu.VMEM((a_count * b_count, pairs), F32),
            pltpu.VMEM((rows_n, few, pairs), F32),
            pltpu.VMEM((slots, take, b_count, group, lanes), F32),
            pltpu.VMEM((slots, take, b_count, group, tail), F32),
            pltpu.VMEM(e.shape[:3] + (lanes,), F32),
            pltpu.VMEM(e.shape[:3] + (tail,), F32),
            pltpu.VMEM((few * c_count, lanes), F32),
            pltpu.VMEM((few, width), BF16),
            pltpu.VMEM((few, width), BF16),
            pltpu.VMEM((few, pairs), F32),
            pltpu.VMEM((cols_n, few, pairs), F32),
            pltpu.VMEM((rows * group, lanes), F32),
            pltpu.VMEM((rows, width), BF16),
            pltpu.VMEM((rows, width), BF16),
            pltpu.VMEM((late, pairs, width), BF16),
            pltpu.VMEM((late, pairs, width), BF16),
            pltpu.VMEM((pairs // lanes, a_count * c_count, lanes), F32),
            pltpu.VMEM((blocks, cols_n, rows_n) + block, F32),
            pltpu.VMEM((blocks, rows_n, 2) + block, F32),
            pltpu.VMEM((blocks, rows_n) + block, F32),
            pltpu.VMEM((blocks, rows_n) + block, F32),
            pltpu.VMEM((blocks, rows_n) + block, F32),
            pltpu.VMEM((blocks, 2, cols_n) + block, F32),
            dma((slots, 2)), dma((chunks + 2,)),
            dma((chunks, cols_n)), dma((chunks, cols_n)),
            dma((chunks, levels)), dma((chunks, levels)),
            dma((chunks, levels)), dma((chunks, levels)),
            dma((chunks, levels)), dma((chunks, levels)),
            dma((cols_n,)), dma((cols_n,)),
            dma((rows_n,)), dma((rows_n,)),
            dma((blocks, rows_n, 2)), dma((blocks, rows_n, 2)),
            dma((blocks, rows_n)), dma((blocks, rows_n)),
            dma((blocks, rows_n)), dma((blocks, rows_n)),
            dma((blocks, rows_n)), dma((blocks, 2, cols_n)),
            dma((blocks, 2, cols_n, 2)), dma((blocks, rows_n, 2)),
            dma((blocks, 5)),
        ],
        compiler_params=pltpu.CompilerParams(
            collective_id=0, has_side_effects=True, vmem_limit_bytes=62 << 20
        ),
    )(x, v, e, known, move)


def fast(amplitudes, vvvv, hole_ints, exchange_ints, fock_occ, fock_vir, eps_occ, eps_vir):
    high = lax.Precision.HIGH
    rows_n = lax.axis_size("row")
    cols_n = lax.axis_size("col")
    row = lax.axis_index("row")
    col = lax.axis_index("col")
    first, second, virtual = amplitudes.shape[:3]
    occupied = fock_occ.shape[0]
    pairs = occupied * occupied
    a_count, c_count = vvvv.shape[0], vvvv.shape[2]
    group, lanes = 8, 128
    tail = virtual - lanes
    chunks = c_count // group
    n = first * second

    half = second // 2
    x = amplitudes.reshape(first, 2, half, virtual, virtual).transpose(1, 0, 2, 3, 4)
    x = x.reshape(n, cols_n, chunks, group, virtual)
    x = jnp.concatenate(
        [
            x[..., :lanes].reshape(n, cols_n, chunks, group * lanes),
            x[..., lanes:].reshape(n, cols_n, chunks, group * tail),
        ],
        axis=-1,
    ).transpose(1, 2, 0, 3)
    delta = jnp.eye(occupied, dtype=fock_occ.dtype)
    known = hole_ints - delta[:, None, :, None] * fock_occ[None, :, None, :]
    highest = lax.Precision.HIGHEST
    one, two = jnp.divmod(jnp.arange(pairs, dtype=jnp.int32), occupied)

    def place(i, j):
        inner = (j % second) // half * (first * half) + (i % first) * half + j % half
        return ((i // first) * cols_n + j // second) * n + inner

    spots = jnp.arange(pairs, dtype=jnp.int32)
    turn = (place(one, two)[:, None] == spots[None, :]).astype(F32)
    move = (spots[:, None] == place(two, one)[None, :]).astype(F32)
    known = jnp.dot(known.reshape(pairs, pairs), turn, precision=highest)


    straight, turned = whole(x, vvvv, exchange_ints, known, move.astype(BF16), rows_n, 4, 3, 2)
    blocks = a_count // 4
    straight = straight.reshape(rows_n, blocks, 2, first, half, 4, virtual)
    straight = straight.transpose(3, 2, 4, 0, 1, 5, 6).reshape(first, second, virtual, virtual)
    turned = turned.reshape(rows_n, blocks, 2, half, first, 4, virtual)
    turned = turned.transpose(4, 2, 3, 6, 0, 1, 5).reshape(first, second, virtual, virtual)
    return close(straight + turned, amplitudes, fock_vir, eps_occ, eps_vir)


def on_device(amplitudes, vvvv, *rest):
    virtual, b_count, c_count = amplitudes.shape[2], vvvv.shape[1], vvvv.shape[2]
    tail = virtual - 128
    fits = (
        virtual > 128
        and 128 % tail == 0
        and c_count % 8 == 0
        and c_count >= 24
        and (c_count // 8 - 2) * (vvvv.shape[0] // 4) >= (c_count // 8 - 1) * (lax.axis_size("row") // 2 - 1)
        and (8 * tail) % 128 == 0
        and vvvv.shape[0] % 4 == 0
        and (4 * b_count) % 128 == 0
        and (amplitudes.shape[0] * amplitudes.shape[1]) % 8 == 0
        and amplitudes.shape[1] == 2 * amplitudes.shape[0]
        and lax.axis_size("row") == 2 * lax.axis_size("col")
        and lax.axis_size("col") == 4
    )
    return (fast if fits else plain)(amplitudes, vvvv, *rest)


def solution(mesh):
    in_specs = (
        P("row", "col", None, None),
        P("row", None, "col", None),
        P(),
        P("row", None, "col", None),
        P(),
        P(),
        P(),
        P(),
    )
    out_specs = P("row", "col", None, None)
    return jax.shard_map(
        on_device, mesh=mesh, in_specs=in_specs, out_specs=out_specs, check_vma=False
    )
```

time: 450 us -> 170 us (0.38)
  waiting for transfers between devices: 176 us -> 0 us
  local copies, waits for them, and re-layouts: 135 us -> 13.2 us
  Pallas kernels: 79.5 us -> 148 us
  blocking collectives: 13.4 us -> 0 us
  between operations: 13.4 us -> 0.13 us
  starting transfers between devices: 11.4 us -> 0 us
  other arithmetic: 13 us -> 2.04 us
    pallas_call x2 -> x1, Pallas kernels: 79.5 us -> 148 us  [whole(): pl.pallas_call(functools.partial(whole_kernel, take, slots, late), out_sh...]
    all_gather x2 -> x0, waiting for transfers between devices: 61.9 us -> none  [the longest x1 61.9 us: fast(): t = lax.all_gather(x, 'row', axis=0)]
    dynamic_update_slice x1 -> x0, local copies, waits for them, and re-layouts: 54.8 us -> none  [fast(): part = lax.dynamic_update_slice_in_dim(part, spot, col * c_count, axis=3)]
    ppermute x2 -> x0, waiting for transfers between devices: 50.4 us -> none  [finish(): others.append(lax.ppermute(block, ('row', 'col'), route))]
    unnamed x4 -> x0, waiting for transfers between devices: 43.3 us -> none
    reshape x9 -> x6, local copies, waits for them, and re-layouts: 38.9 us -> 9.98 us  [the longest x2 3.05 us: fast(): turned = turned.reshape(rows_n, blocks, 2, half, first, 4, virtual)]
    all_to_all x1 -> x0, waiting for transfers between devices: 20.4 us -> none  [fast(): raw = lax.all_to_all(raw, 'row', split_axis=0, concat_axis=0, tiled=True)]
    transpose x3 -> x2, local copies, waits for them, and re-layouts: 19.6 us -> 1.72 us  [the longest x1 1.48 us: fast(): amplitudes.reshape(first, 2, half, virtual, virtual)]
  transfers between devices with their start and end apart: 6 -> 0, of which waited for: 5 -> 0; matrix products, arithmetic and copies ran while one was open for 5% -> 0% of each run, Pallas kernels for 16% -> 0%
where the time goes in v4:
time: 170 us; the launch traced here: 169 us
  Pallas kernels  148 us (87%)
  local copies, waits for them, and re-layouts  13.2 us (8%)
  matrix products  5.35 us (3%)
  other arithmetic  2.04 us (1%)
    pallas_call x1, Pallas kernels, whole(): pl.pallas_call(functools.partial(whole_kernel, take, slots, late), out_sh...  148 us

profile of v4, /device:TPU:3, one launch (start us, length us, event | category | flops | bytes accessed | tf_op | source)
XLA Modules:
  0.0 169.1 jit_solution(5991857536484671990)
XLA Ops:
  0.0 1.5 copy.20
  1.6 0.2 reshape.298
  1.8 0.1 copy.31
  2.0 0.0 copy-start.2
  2.0 0.4 copy.33
  2.4 0.9 maximum_bitcast_fusion.x_ref
  3.3 0.5 copy-done.2
  3.9 0.2 multiply_subtract_fusion
  4.1 0.9 reshape.292
  5.0 1.1 fusion.2.known_ref
  6.1 0.7 convert_convert_fusion.move_ref
  6.8 148.4 %shard_map.82 = (f32[8,5,2,4,640]{4,3,2,1,0:T(4,128)}, f32[8,5,2,4,640]{4,3,2,1,0:T(4,128)}) custom-call(f32[4,5,8,1280]{3,2,1,0:T(8,128)} %maximum_bitcast_fusion.x_ref, f32[20,160,40,160]{3,2,1,0:T(8,128)} %v_ref.1, f32[2,16,40,160]{3,2,1,0:T(8,128)} %e_ref.1, f32[256,256]{1,0:T(8,128)} %fusion.2.known_ref, bf16[256,256]{1,0:T(8,128)(2,1)} %convert_convert_fusion.move_ref), custom_call_target="tpu_custom_call" | custom-call | tf_op jit(solution)/shard_map/pallas_call | solution.py:635
  155.2 2.4 %reshape.293 = f32[8,5,2,2,2,4,160]{6,5,4,3,2,1,0:T(4,128)S(1)} reshape(f32[8,5,2,4,640]{4,3,2,1,0:T(4,128)} %get-tuple-element.7) | data formatting | bytes 1638400 | tf_op jit(solution)/shard_map/reshape | solution.py:727
  157.6 0.2 copy.23
  157.8 1.5 reshape.294
  159.3 2.4 %reshape.295 = f32[8,5,2,2,2,4,160]{6,5,4,3,2,1,0:T(4,128)S(1)} reshape(f32[8,5,2,4,640]{4,3,2,1,0:T(4,128)} %get-tuple-element.8) | data formatting | bytes 1638400 | tf_op jit(solution)/shard_map/reshape | solution.py:729
  161.7 0.7 copy.24
  162.4 2.1 %copy.25 = f32[2,4,160,160]{3,2,1,0:T(8,128)} copy(f32[2,4,160,160]{2,0,3,1:T(2,128)S(1)} %bitcast.36) | data formatting | bytes 1638400 | tf_op jit(solution)/shard_map/reshape | solution.py:730
  164.5 2.4 %convolution_add_fusion = f32[2,4,160,160]{3,2,1,0:T(8,128)S(1)} fusion(f32[2,4,160,160]{3,2,1,0:T(8,128)S(1)} %copy-done.1, f32[2,4,160,160]{3,2,1,0:T(8,128)} %reshape.294, f32[2,4,160,160]{3,2,1,0:T(8,128)} %copy.25, f32[160,160]{1,0:T(8,128)S(1)} %copy-done), kind=kOutput, calls=%fused_computation.4 | convolution fusion | flops 197017600 | bytes 3379200 | tf_op jit(solution)/shard_map/ijac,cb->ijab/dot_general | solution.py:42
  166.9 0.1 dynamic_slice.7
  167.0 0.1 dynamic_slice.6
  167.1 0.1 broadcast_add_fusion
  167.2 0.1 broadcast_subtract_fusion
  167.2 1.9 %fusion.1 = f32[2,4,160,160]{3,2,1,0:T(8,128)} fusion(f32[2,4,160,160]{3,2,1,0:T(8,128)S(1)} %convolution_add_fusion, f32[2,4,160,160]{3,2,1,0:T(8,128)S(1)} %copy-done.1, f32[160]{0:T(256)S(1)} %copy-done.4, f32[2,4,160]{2,1,0:T(4,128)S(1)} %broadcast_subtract_fusion, f32[160,160]{1,0:T(8,128)S(1)} %copy-done), kind=kOutput, calls=%fused_computation.3 | convolution fusion | flops 197222400 | bytes 2565760 | tf_op jit(solution)/shard_map/ac,ijcb->ijab/dot_general | solution.py:43
  (15 shorter events, 0.2 us)
Async XLA Ops:
  0.0 164.5 %copy-start = (f32[160,160]{1,0:T(8,128)S(1)}, f32[160,160]{1,0:T(8,128)}, u32[]{:S(2)}) copy-start(f32[160,160]{1,0:T(8,128)} %param.13) | copy-start | bytes 307204
  2.0 1.9 %copy-start.2 = (f32[16,16,16,16]{3,2,1,0:T(8,128)S(1)}, f32[16,16,16,16]{3,2,1,0:T(8,128)}, u32[]{:S(2)}) copy-start(f32[16,16,16,16]{3,2,1,0:T(8,128)} %param.10) | copy-start | bytes 786436
  2.0 1.9 %copy-start.3 = (f32[16,16]{1,0:T(8,128)S(1)}, f32[16,16]{1,0:T(8,128)}, u32[]{:S(2)}) copy-start(f32[16,16]{1,0:T(8,128)} %param.12) | copy-start | bytes 3076
  162.4 2.1 %copy-start.1 = (f32[2,4,160,160]{3,2,1,0:T(8,128)S(1)}, f32[2,4,160,160]{3,2,1,0:T(8,128)}, u32[]{:S(2)}) copy-start(f32[2,4,160,160]{3,2,1,0:T(8,128)} %param.8) | copy-start | bytes 2457604
  164.5 2.4 %copy-start.5 = (f32[16]{0:T(128)S(1)}, f32[16]{0:T(128)}, u32[]{:S(2)}) copy-start(f32[16]{0:T(128)} %param.14) | copy-start | bytes 196
  164.5 2.7 %copy-start.4 = (f32[160]{0:T(256)S(1)}, f32[160]{0:T(256)}, u32[]{:S(2)}) copy-start(f32[160]{0:T(256)} %param.15) | copy-start | bytes 1924

commit v5 on v4

--- a/solution.py
+++ b/solution.py
@@ -2,6 +2,7 @@
 
 import jax
 import jax.numpy as jnp
+import numpy as np
 from jax import lax
 from jax.experimental import pallas as pl
 from jax.experimental.pallas import tpu as pltpu
@@ -496,16 +497,19 @@
 
     def opening(step, _):
         chunk, block = step // blocks, lax.rem(step, blocks)
-        ahead = 1 + step // (levels - 1)
-
-        @pl.when(ahead < chunks)
+        count = early * blocks
+        events = (chunks - 1) * (levels - 1)
+        event = (step * events + count - 1) // count
+        ahead = 1 + event // (levels - 1)
+
+        @pl.when((event * count // events == step) & (event < events))
         def _():
             for k in range(1, levels):
-                @pl.when(lax.rem(step, levels - 1) == k - 1)
+                @pl.when(lax.rem(event, levels - 1) == k - 1)
                 def _():
                     relay(k, ahead)
 
-            @pl.when((lax.rem(step, levels - 1) == 0) & (ahead + 1 < chunks))
+            @pl.when((lax.rem(event, levels - 1) == 0) & (ahead + 1 < chunks))
             def _():
                 open_up(ahead + 1)
 
@@ -710,19 +714,20 @@
     delta = jnp.eye(occupied, dtype=fock_occ.dtype)
     known = hole_ints - delta[:, None, :, None] * fock_occ[None, :, None, :]
     highest = lax.Precision.HIGHEST
-    one, two = jnp.divmod(jnp.arange(pairs, dtype=jnp.int32), occupied)
+    one, two = np.divmod(np.arange(pairs), occupied)
 
     def place(i, j):
         inner = (j % second) // half * (first * half) + (i % first) * half + j % half
         return ((i // first) * cols_n + j // second) * n + inner
 
-    spots = jnp.arange(pairs, dtype=jnp.int32)
-    turn = (place(one, two)[:, None] == spots[None, :]).astype(F32)
-    move = (spots[:, None] == place(two, one)[None, :]).astype(F32)
+    spots = np.arange(pairs)
+    turn = jnp.asarray((place(one, two)[:, None] == spots[None, :]).astype(np.float32))
+    move = jnp.asarray((spots[:, None] == place(two, one)[None, :]).astype(np.float32), BF16)
+
     known = jnp.dot(known.reshape(pairs, pairs), turn, precision=highest)
 
 
-    straight, turned = whole(x, vvvv, exchange_ints, known, move.astype(BF16), rows_n, 4, 3, 2)
+    straight, turned = whole(x, vvvv, exchange_ints, known, move, rows_n, 4, 3, 2)
     blocks = a_count // 4
     straight = straight.reshape(rows_n, blocks, 2, first, half, 4, virtual)
     straight = straight.transpose(3, 2, 4, 0, 1, 5, 6).reshape(first, second, virtual, virtual)

time: 170 us -> 168 us (0.988)
  no operation moved by 1% of the time
where the time goes in v5:
time: 168 us; the launch traced here: 167 us
  Pallas kernels  147 us (88%)
  local copies, waits for them, and re-layouts  13.2 us (8%)
  matrix products  5.37 us (3%)
    pallas_call x1, Pallas kernels, whole(): pl.pallas_call(functools.partial(whole_kernel, take, slots, late), out_sh...  147 us

profile of v5, /device:TPU:3, one launch (start us, length us, event | category | flops | bytes accessed | tf_op | source)
XLA Modules:
  0.0 167.0 jit_solution(11239399223295258523)
XLA Ops:
  0.0 1.5 copy.22
  1.6 0.2 reshape.86
  1.8 0.1 copy.33
  2.0 0.0 copy-start.2
  2.0 0.4 copy.35
  2.4 0.9 maximum_bitcast_fusion.x_ref
  3.3 0.5 copy-done.2
  3.9 0.2 multiply_subtract_fusion
  4.1 0.0 copy-start.3
  4.1 0.9 reshape.80
  5.1 1.1 fusion.5.known_ref
  6.1 146.9 %shard_map.100 = (f32[8,5,2,4,640]{4,3,2,1,0:T(4,128)}, f32[8,5,2,4,640]{4,3,2,1,0:T(4,128)}) custom-call(f32[4,5,8,1280]{3,2,1,0:T(8,128)} %maximum_bitcast_fusion.x_ref, f32[20,160,40,160]{3,2,1,0:T(8,128)} %v_ref.1, f32[2,16,40,160]{3,2,1,0:T(8,128)} %e_ref.1, f32[256,256]{1,0:T(8,128)} %fusion.5.known_ref, bf16[256,256]{1,0:T(8,128)(2,1)} %constant.22.clone.move_ref), custom_call_target="tpu_custom_call" | custom-call | tf_op jit(solution)/shard_map/pallas_call | solution.py:639
  153.1 2.4 %reshape.81 = f32[8,5,2,2,2,4,160]{6,5,4,3,2,1,0:T(4,128)S(1)} reshape(f32[8,5,2,4,640]{4,3,2,1,0:T(4,128)} %get-tuple-element.7) | data formatting | bytes 1638400 | tf_op jit(solution)/shard_map/reshape | solution.py:732
  155.4 0.2 copy.25
  155.7 1.5 reshape.82
  157.2 2.4 %reshape.83 = f32[8,5,2,2,2,4,160]{6,5,4,3,2,1,0:T(4,128)S(1)} reshape(f32[8,5,2,4,640]{4,3,2,1,0:T(4,128)} %get-tuple-element.8) | data formatting | bytes 1638400 | tf_op jit(solution)/shard_map/reshape | solution.py:734
  159.6 0.7 copy.26
  160.3 2.1 %copy.27 = f32[2,4,160,160]{3,2,1,0:T(8,128)} copy(f32[2,4,160,160]{2,0,3,1:T(2,128)S(1)} %bitcast.37) | data formatting | bytes 1638400 | tf_op jit(solution)/shard_map/reshape | solution.py:735
  162.4 2.4 %convolution_add_fusion = f32[2,4,160,160]{3,2,1,0:T(8,128)S(1)} fusion(f32[2,4,160,160]{3,2,1,0:T(8,128)S(1)} %copy-done.1, f32[2,4,160,160]{3,2,1,0:T(8,128)} %reshape.82, f32[2,4,160,160]{3,2,1,0:T(8,128)} %copy.27, f32[160,160]{1,0:T(8,128)S(1)} %copy-done), kind=kOutput, calls=%fused_computation.4 | convolution fusion | flops 197017600 | bytes 3379200 | tf_op jit(solution)/shard_map/ijac,cb->ijab/dot_general | solution.py:43
  164.8 0.1 dynamic_slice.7
  164.9 0.1 dynamic_slice.6
  165.0 0.1 broadcast_add_fusion
  165.0 0.1 broadcast_subtract_fusion
  165.1 1.9 %fusion.1 = f32[2,4,160,160]{3,2,1,0:T(8,128)} fusion(f32[2,4,160,160]{3,2,1,0:T(8,128)S(1)} %convolution_add_fusion, f32[2,4,160,160]{3,2,1,0:T(8,128)S(1)} %copy-done.1, f32[160]{0:T(256)S(1)} %copy-done.5, f32[2,4,160]{2,1,0:T(4,128)S(1)} %broadcast_subtract_fusion, f32[160,160]{1,0:T(8,128)S(1)} %copy-done), kind=kOutput, calls=%fused_computation.3 | convolution fusion | flops 197222400 | bytes 2565760 | tf_op jit(solution)/shard_map/ac,ijcb->ijab/dot_general | solution.py:44
  (14 shorter events, 0.1 us)
Async XLA Ops:
  0.0 162.4 %copy-start = (f32[160,160]{1,0:T(8,128)S(1)}, f32[160,160]{1,0:T(8,128)}, u32[]{:S(2)}) copy-start(f32[160,160]{1,0:T(8,128)} %param.15) | copy-start | bytes 307204
  2.0 1.9 %copy-start.2 = (f32[16,16,16,16]{3,2,1,0:T(8,128)S(1)}, f32[16,16,16,16]{3,2,1,0:T(8,128)}, u32[]{:S(2)}) copy-start(f32[16,16,16,16]{3,2,1,0:T(8,128)} %param.12) | copy-start | bytes 786436
  2.0 1.9 %copy-start.4 = (f32[16,16]{1,0:T(8,128)S(1)}, f32[16,16]{1,0:T(8,128)}, u32[]{:S(2)}) copy-start(f32[16,16]{1,0:T(8,128)} %param.14) | copy-start | bytes 3076
  4.1 1.0 copy-start.3
  160.3 2.1 %copy-start.1 = (f32[2,4,160,160]{3,2,1,0:T(8,128)S(1)}, f32[2,4,160,160]{3,2,1,0:T(8,128)}, u32[]{:S(2)}) copy-start(f32[2,4,160,160]{3,2,1,0:T(8,128)} %param.10) | copy-start | bytes 2457604
  162.4 2.4 %copy-start.6 = (f32[16]{0:T(128)S(1)}, f32[16]{0:T(128)}, u32[]{:S(2)}) copy-start(f32[16]{0:T(128)} %param.16) | copy-start | bytes 196
  162.4 2.7 %copy-start.5 = (f32[160]{0:T(256)S(1)}, f32[160]{0:T(256)}, u32[]{:S(2)}) copy-start(f32[160]{0:T(256)} %param.17) | copy-start | bytes 1924
